TPU v7x, 256 devices: a whole 4x4x8 slice. The times are simulated.
256 devices in a mesh: ctx: 32 (over z_hi, x, y), fsdp: 8 (over z_lo, core).
Axes of the slice: x: 4, y: 4, z: 8 (z_hi: 2, z_lo: 4; z = z_hi * 4 + z_lo), core: 2. Of those that a mesh axis runs over, the one named last changes fastest.
Arguments:
- out_grad: bfloat16 [4096, 32768], P('fsdp', 'ctx'), may hold values from -6 to 6
- gate_values: bfloat16 [4096, 32768], P('fsdp', 'ctx'), may hold values from -6 to 6
- kv_product: bfloat16 [4096, 32768], P('fsdp', 'ctx'), may hold values from -6 to 6
- w_out: bfloat16 [4096, 4096], P('ctx', 'fsdp'), may hold values from -0.09375 to 0.09375
- filters: bfloat16 [8, 32, 16, 128], P('fsdp', 'ctx'), may hold values from -0.5 to 0.5
Outputs:
- gate_grad: float32 [4096, 32768], P('fsdp', 'ctx')
- kv_grad: bfloat16 [4096, 32768], P('fsdp', 'ctx')
- filter_grad: float32 [8, 32, 16, 128], P('fsdp', 'ctx')
- w_grad: float32 [4096, 4096], P('ctx', 'fsdp')
All inputs are finite; a program needn't handle non-finite values.
Results may differ from a plain program's by a relative error of at most 0.0049.
Values may be sent and summed in bfloat16 or wider, within the bound.
A program may use at most 128 MiB of HBM per device.

v0:
```python
import math

import jax
import jax.numpy as jnp
from jax import lax
from jax.sharding import PartitionSpec as P


def toeplitz_pair(filters):
    channels, tap_count = filters.shape
    zero_pad = jnp.zeros_like(filters)

    def make_band(vector):
        tiled = jnp.tile(vector, (1, tap_count + 1))
        window_cut = tiled[:, tap_count : tap_count + tap_count * (2 * tap_count - 1)]
        return window_cut.reshape(channels, tap_count, 2 * tap_count - 1)[:, :, :tap_count]

    near_band = make_band(jnp.concatenate([zero_pad, filters], axis=1))
    far_band = make_band(jnp.concatenate([filters, zero_pad], axis=1))
    return (near_band, far_band)


def mixer_piece(filters, signal, signal_prior, cotangent, cotangent_after):
    channels, seq_len = signal.shape
    tap_count = filters.shape[1]
    blocks_count = seq_len // tap_count
    near_band, far_band = toeplitz_pair(filters)
    current = signal.reshape(channels, blocks_count, tap_count)
    previous = jnp.concatenate([signal_prior[:, None, :], current[:, :-1]], axis=1)
    grad_current = cotangent.reshape(channels, blocks_count, tap_count)
    grad_later = jnp.concatenate([grad_current[:, 1:], cotangent_after[:, None, :]], axis=1)
    wide = jnp.float32
    mixed = jnp.einsum("cbs,csr->cbr", current, near_band, preferred_element_type=wide)
    mixed = mixed + jnp.einsum("cbs,csr->cbr", previous, far_band, preferred_element_type=wide)
    signal_grad = jnp.einsum("cbr,csr->cbs", grad_current, near_band, preferred_element_type=wide)
    signal_grad = signal_grad + jnp.einsum(
        "cbr,csr->cbs", grad_later, far_band, preferred_element_type=wide
    )
    near_weight = jnp.einsum("cbs,cbr->csr", current, grad_current, preferred_element_type=wide)
    far_weight = jnp.einsum("cbs,cbr->csr", previous, grad_current, preferred_element_type=wide)
    band_pair, pullback = jax.vjp(toeplitz_pair, filters.astype(jnp.float32))
    filter_part = pullback((near_weight, far_weight))[0]
    return (mixed.reshape(channels, seq_len), signal_grad.reshape(channels, seq_len), filter_part)


def on_device(out_grad, gate_values, kv_product, w_out, filters):
    ctx_count = lax.axis_size("ctx")
    chan_count = filters.shape[2]
    tap_count = filters.shape[3]
    norm_scale = 1.0 / math.sqrt(ctx_count * out_grad.shape[1])
    grad_full = lax.all_gather(out_grad, "fsdp", axis=0, tiled=True)
    grad_part = grad_full
    mix_grad = lax.dot_general(
        lax.all_gather(w_out, "ctx", axis=0, tiled=True),
        grad_part,
        (((0,), (0,)), ((), ())),
        preferred_element_type=jnp.float32,
    )
    conv_grad = (mix_grad * gate_values.astype(jnp.float32)).astype(jnp.bfloat16)
    signal_chan, grad_chan = (
        lax.all_to_all(kv_product, "ctx", split_axis=0, concat_axis=1, tiled=True),
        lax.all_to_all(conv_grad, "ctx", split_axis=0, concat_axis=1, tiled=True),
    )
    own_filters = filters.reshape(chan_count, tap_count)
    edge_zero = jnp.zeros((chan_count, tap_count), jnp.bfloat16)
    mixed, signal_grad, filter_part = mixer_piece(
        own_filters, signal_chan, edge_zero, grad_chan, edge_zero
    )
    mixed_tok, kv_grad = (
        lax.all_to_all(mixed.astype(jnp.bfloat16), "ctx", split_axis=1, concat_axis=0, tiled=True),
        lax.all_to_all(
            signal_grad.astype(jnp.bfloat16), "ctx", split_axis=1, concat_axis=0, tiled=True
        ),
    )
    filter_grad = (filter_part * norm_scale).reshape(filters.shape)
    mixed_wide = mixed_tok.astype(jnp.float32)
    gate_grad = mix_grad * mixed_wide
    gated_rows = (gate_values.astype(jnp.float32) * mixed_wide).astype(jnp.bfloat16)
    grad_part = grad_full
    w_grad = (
        lax.psum_scatter(
            lax.dot_general(
                grad_part, gated_rows, (((1,), (1,)), ((), ())), preferred_element_type=jnp.float32
            ),
            "ctx",
            scatter_dimension=0,
            tiled=True,
        )
        * norm_scale
    )
    return (gate_grad, kv_grad, filter_grad, w_grad)


def solution(mesh):
    in_specs = (
        P("fsdp", "ctx"),
        P("fsdp", "ctx"),
        P("fsdp", "ctx"),
        P("ctx", "fsdp"),
        P("fsdp", "ctx", None, None),
    )
    out_specs = (P("fsdp", "ctx"), P("fsdp", "ctx"), P("fsdp", "ctx", None, None), P("ctx", "fsdp"))
    return jax.shard_map(
        on_device, mesh=mesh, in_specs=in_specs, out_specs=out_specs, check_vma=False
    )
```

profile of v0, /device:TPU:32, one launch (start us, length us, event | category | flops | bytes accessed | tf_op | source)
XLA Modules:
  0.0 575.9 jit_solution(2997700983290757412)
XLA Ops:
  8.7 13.1 %all-to-all-start = ((bf16[32,16,1024]{2,1,0:T(8,128)(2,1)}), bf16[32,16,1024]{2,1,0:T(8,128)(2,1)S(1)}, u32[]{:S(2)}, u32[]{:S(2)}) async-start(bf16[32,16,1024]{2,1,0:T(8,128)(2,1)} %bitcast.45), calls=%async_computation | async-start | bytes 2097152 | tf_op jit(solution)/shard_map/all_to_all | solution.py:61
  22.2 3.4 reshape.73
  26.9 4.6 reshape.71
  31.5 23.4 %all-to-all-done = bf16[32,16,1024]{2,1,0:T(8,128)(2,1)S(1)} async-done(((bf16[32,16,1024]{2,1,0:T(8,128)(2,1)}), bf16[32,16,1024]{2,1,0:T(8,128)(2,1)S(1)}, u32[]{:S(2)}, u32[]{:S(2)}) %all-to-all-start) | async-done | bytes 1048608 | tf_op jit(solution)/shard_map/all_to_all | solution.py:61
  55.0 1.5 copy.30
  56.5 1.5 reshape.72
  58.6 1.5 fusion.2
  60.0 1.6 copy.32
  62.9 1.8 copy.33
  64.7 31.7 %all_to_all.58 = bf16[16,32,1024]{2,0,1:T(8,128)(2,1)} all-to-all(bf16[16,32,1024]{2,0,1:T(8,128)(2,1)S(1)} %copy.33), channel_id=1, replica_groups=mesh['ctx'=32,'fsdp'=8] {'ctx'}, dimensions={1} | all-to-all | bytes 2097152 | tf_op jit(solution)/shard_map/all_to_all | solution.py:70
  96.5 51.4 %all-gather.3.cloned.1.call-done = bf16[4096,512]{1,0:T(8,128)(2,1)} async-done(((bf16[128,512]{1,0:T(8,128)(2,1)}), bf16[4096,512]{1,0:T(8,128)(2,1)}) %all-gather.3.cloned.1.call-update) | async-done | bytes 4194320 | tf_op jit(solution)/shard_map/all_gather | solution.py:54
  147.9 86.7 %all-gather.5.cloned.1.call-done = bf16[4096,1024]{1,0:T(8,128)(2,1)} async-done(((bf16[512,1024]{1,0:T(8,128)(2,1)}), bf16[4096,1024]{1,0:T(8,128)(2,1)}) %all-gather.5.cloned.1.call-update) | async-done | bytes 8388624 | tf_op jit(solution)/shard_map/all_gather | solution.py:51
  234.6 11.6 %fusion = (bf16[512,1024]{1,0:T(8,128)(2,1)}, f32[512,1024]{1,0:T(8,128)}, bf16[512,1024]{1,0:T(8,128)(2,1)S(1)}) fusion(bf16[512,1024]{1,0:T(8,128)(2,1)} %param.6, bf16[16,32,1024]{2,0,1:T(8,128)(2,1)} %all_to_all.58, bf16[4096,512]{1,0:T(8,128)(2,1)} %all-gather.3.cloned.1.call-done, bf16[4096,1024]{1,0:T(8,128)(2,1)} %all-gather.5.cloned.1.call-done), kind=kOutput, calls=%fused_computation.3 | convolution fusion | flops 4298637312 | bytes 18874368 | tf_op jit(solution)/shard_map/dot_general | solution.py:53
  246.2 6.9 %convolution_bitcast_fusion = f32[4096,512]{0,1:T(8,128)} fusion(bf16[512,1024]{1,0:T(8,128)(2,1)S(1)} %get-tuple-element.18, bf16[4096,1024]{1,0:T(8,128)(2,1)S(1)} %copy-done.3), kind=kOutput, calls=%fused_computation | convolution fusion | flops 4294967296 | bytes 17825792 | tf_op jit(solution)/shard_map/dot_general | solution.py:82
  253.1 59.1 %all_to_all.59 = bf16[32,16,1024]{2,1,0:T(8,128)(2,1)S(1)} all-to-all(bf16[32,16,1024]{2,1,0:T(8,128)(2,1)} %bitcast.46), channel_id=1, replica_groups=mesh['ctx'=32,'fsdp'=8] {'ctx'}, dimensions={0} | all-to-all | bytes 2097152 | tf_op jit(solution)/shard_map/all_to_all | solution.py:62
  312.2 1.5 copy.34
  313.7 1.5 reshape.74
  316.9 1.4 add_convert_fusion
  318.4 1.5 convert_element_type.41
  319.9 1.5 copy.36
  321.4 5.2 all-to-all-start.3
  328.5 2.8 pad.18.clone
  331.3 4.2 reshape.77
  335.4 3.0 pad.19
  338.5 2.9 reshape.78
  341.3 1.8 reduce_sum.19
  343.9 2.6 reshape.75
  346.5 3.1 pad.17
  349.5 1.7 reshape.76
  352.1 3.0 all-to-all-done.3
  355.0 210.2 %reduce-scatter.2.cloned.1.call-done = f32[128,512]{0,1:T(8,128)} async-done(((f32[4096,512]{0,1:T(8,128)}), f32[128,512]{0,1:T(8,128)}) %reduce-scatter.2.cloned.1.call-update) | async-done | bytes 262160 | tf_op jit(solution)/shard_map/reduce_scatter | solution.py:81
  567.1 2.3 copy.50
  (33 shorter events, 11.8 us)
Async XLA Ops:
  7.2 14.6 %copy-start.2 = (bf16[1,1,16,128]{3,2,1,0:T(8,128)(2,1)S(1)}, bf16[1,1,16,128]{3,2,1,0:T(8,128)(2,1)}, u32[]{:S(2)}) copy-start(bf16[1,1,16,128]{3,2,1,0:T(8,128)(2,1)} %param.9) | copy-start | bytes 12292
  7.2 140.7 %all-gather.3.cloned.1.call-start = ((), (), s32[]{:S(2)}) async-start(), calls=%async_computation.5 | async-start | bytes 4325376 | tf_op jit(solution)/shard_map/all_gather | solution.py:54
  7.9 226.7 %all-gather.5.cloned.1.call-start = ((), (), s32[]{:S(2)}) async-start(), calls=%async_computation.6 | async-start | bytes 9437184 | tf_op jit(solution)/shard_map/all_gather | solution.py:51
  8.7 46.3 %all-to-all-start = ((bf16[32,16,1024]{2,1,0:T(8,128)(2,1)}), bf16[32,16,1024]{2,1,0:T(8,128)(2,1)S(1)}, u32[]{:S(2)}, u32[]{:S(2)}) async-start(bf16[32,16,1024]{2,1,0:T(8,128)(2,1)} %bitcast.45), calls=%async_computation | async-start | bytes 2097152 | tf_op jit(solution)/shard_map/all_to_all | solution.py:61
  21.7 543.6 %reduce-scatter.2.cloned.1.call-start = ((), (), s32[]{:S(2)}) async-start(), calls=%async_computation.7 | async-start | bytes 8650752 | tf_op jit(solution)/shard_map/reduce_scatter | solution.py:81
  31.5 27.0 %copy-start = (bf16[16,128,255]{2,1,0:T(8,128)(2,1)}, bf16[16,128,255]{2,1,0:T(8,128)(2,1)S(1)}, u32[]{:S(2)}) copy-start(bf16[16,128,255]{2,1,0:T(8,128)(2,1)S(1)} %reshape.71) | copy-start | bytes 3133444
  234.6 11.6 %copy-start.3 = (bf16[4096,1024]{1,0:T(8,128)(2,1)S(1)}, bf16[4096,1024]{1,0:T(8,128)(2,1)}, u32[]{:S(2)}) copy-start(bf16[4096,1024]{1,0:T(8,128)(2,1)} %all-gather.5.cloned.1.call-done) | copy-start | bytes 25165828
  315.3 1.2 copy-start.1
  321.4 33.6 %all-to-all-start.3 = ((bf16[16,32,1024]{2,0,1:T(8,128)(2,1)}), bf16[16,32,1024]{2,0,1:T(8,128)(2,1)}, u32[]{:S(2)}, u32[]{:S(2)}) async-start(bf16[16,32,1024]{2,0,1:T(8,128)(2,1)} %copy.36), calls=%async_computation.3 | async-start | bytes 2097152 | tf_op jit(solution)/shard_map/all_to_all | solution.py:71
Sparse Core Ops, SparseCore 0:
  11.5 136.3 all-gather.2
  149.7 84.8 all-gather.4
  253.2 312.0 reduce-scatter.1
where the time goes:
time: 577 us; the launch traced here: 576 us
  waiting for transfers between devices  376 us (65%)
  blocking collectives  90.8 us (16%)
  local copies, waits for them, and re-layouts  49.6 us (9%)
  matrix products  23.3 us (4%)
  starting transfers between devices  18.4 us (3%)
  between operations  14 us (2%)
    reduce_scatter x1, waiting for transfers between devices, on_device(): lax.psum_scatter(lax.dot_general(grad_part, gated_rows, (((1,), (1,)), ((...  210 us
    all_gather x1, waiting for transfers between devices, on_device(): grad_full = lax.all_gather(out_grad, 'fsdp', axis=0, tiled=True)  86.7 us
    all_to_all x1, blocking collectives, on_device(): lax.all_to_all(conv_grad, 'ctx', split_axis=0, concat_axis=1, tiled=True)  59.1 us
    all_gather x1, waiting for transfers between devices, on_device(): lax.all_gather(w_out, 'ctx', axis=0, tiled=True)  51.4 us
    all_to_all x1, blocking collectives, on_device(): lax.all_to_all(mixed.astype(jnp.bfloat16), 'ctx', split_axis=1, concat_ax...  31.7 us
    all_to_all x1, waiting for transfers between devices, on_device(): lax.all_to_all(kv_product, 'ctx', split_axis=0, concat_axis=1, tiled=True)  23.4 us
    reshape x4, local copies, waits for them, and re-layouts, make_band(): window_cut.reshape(channels, tap_count, 2 * tap_count - 1)[:, :, :tap_count]  14.7 us
    all_to_all x1, starting transfers between devices, on_device(): lax.all_to_all(kv_product, 'ctx', split_axis=0, concat_axis=1, tiled=True)  13.1 us
  transfers between devices with their start and end apart: 5, of which 5 were waited for; matrix products, arithmetic and copies ran while one was open for 9% of the time, Pallas kernels for 0%

commit v1 on v0

v1 whole, which is shorter than its diff:
```python
import functools
import math

import jax
import jax.numpy as jnp
from jax import lax
from jax.experimental import pallas as pl
from jax.experimental.pallas import tpu as pltpu
from jax.sharding import PartitionSpec as P

F32 = jnp.float32
BF = jnp.bfloat16

def band_pair(row):
    rows = lax.broadcasted_iota(jnp.int32, (128, 128), 0)
    lanes = lax.broadcasted_iota(jnp.int32, (128, 128), 1)
    turned = pltpu.roll(jnp.broadcast_to(row, (128, 128)), 0, 1, stride=1, stride_axis=0)
    near = jnp.where(lanes >= rows, turned, 0.0).astype(BF)
    far = jnp.where(lanes < rows, turned, 0.0).astype(BF)
    return far, near

def conv_group(h16, lhs, swap):
    sub = lax.broadcasted_iota(jnp.int32, (8, 128), 0)
    out = [[None, None] for _ in range(8)]
    for pair in range(8):
        cols = []
        for ch in (2 * pair, 2 * pair + 1):
            far, near = band_pair(h16[ch:ch + 1, :])
            cols.append(jnp.concatenate([far, near] if not swap else [near, far], axis=0))
        w = jnp.concatenate(cols, axis=1)
        r = jnp.dot(lhs, w, preferred_element_type=F32)
        for k in range(2):
            ch = 2 * pair + k
            half = ch // 8
            for b in range(8):
                piece = r[b * 16 + half * 8: b * 16 + half * 8 + 8, k * 128:(k + 1) * 128]
                o = out[b][half]
                out[b][half] = piece if o is None else jnp.where(sub == ch % 8, piece, o)
    return [jnp.concatenate(o, axis=0) for o in out]

def kernel_a(kv_ref, halo_ref, gate_ref, filt_ref, mixed_ref, gated_ref):
    def body(g, _):
        rows = pl.ds(pl.multiple_of(g * 16, 16), 16)
        xs = [halo_ref[rows, :]] + [kv_ref[rows, b * 128:(b + 1) * 128] for b in range(8)]
        lhs = jnp.concatenate([jnp.concatenate([xs[b], xs[b + 1]], axis=1) for b in range(8)], axis=0)
        outs = conv_group(filt_ref[rows, :].astype(F32), lhs, False)
        for b in range(8):
            m = outs[b].astype(BF)
            mixed_ref[rows, b * 128:(b + 1) * 128] = m
            gated_ref[rows, b * 128:(b + 1) * 128] = (gate_ref[rows, b * 128:(b + 1) * 128].astype(F32) * m.astype(F32)).astype(BF)
        return 0
    lax.fori_loop(0, 32, body, 0)

def conv_a(kv, halo, gate, filt):
    return pl.pallas_call(kernel_a, out_shape=[jax.ShapeDtypeStruct(kv.shape, BF)] * 2,
        in_specs=[pl.BlockSpec(memory_space=pltpu.VMEM)] * 4, out_specs=[pl.BlockSpec(memory_space=pltpu.VMEM)] * 2,
        compiler_params=pltpu.CompilerParams(vmem_limit_bytes=48 << 20))(kv, halo, gate, filt)

def kernel_b(kv_ref, halo_ref, cg_ref, after_ref, rfilt_ref, kvg_ref, fg_ref, part):
    rows_i = lax.broadcasted_iota(jnp.int32, (128, 128), 0)
    lanes_i = lax.broadcasted_iota(jnp.int32, (128, 128), 1)
    def body(g, _):
        rows = pl.ds(pl.multiple_of(g * 16, 16), 16)
        xs = [halo_ref[rows, :]] + [kv_ref[rows, b * 128:(b + 1) * 128] for b in range(8)]
        gs = [cg_ref[rows, b * 128:(b + 1) * 128] for b in range(8)] + [after_ref[rows, :]]
        lhs = jnp.concatenate([jnp.concatenate([gs[b], gs[b + 1]], axis=1) for b in range(8)], axis=0)
        hr = rfilt_ref[rows, :].astype(F32)
        sub = lax.broadcasted_iota(jnp.int32, (8, 128), 0)
        out = [[None, None] for _ in range(8)]
        x = jnp.concatenate([jnp.concatenate([xs[b], xs[b + 1]], axis=1) for b in range(8)], axis=0)
        xt = x.astype(F32).T.astype(BF)
        gg = jnp.concatenate(gs[:8], axis=0)
        chan = lax.broadcasted_iota(jnp.int32, (128, 128), 0) % 16
        ggf = gg.astype(F32)
        for pair in range(8):
            cols = []; gcols = []
            for ch in (2 * pair, 2 * pair + 1):
                turned = pltpu.roll(jnp.broadcast_to(hr[ch:ch + 1, :], (128, 128)), 0, 1, stride=1, stride_axis=0)
                near = jnp.where(rows_i >= lanes_i, turned, 0.0).astype(BF)
                far = jnp.where(rows_i < lanes_i, turned, 0.0).astype(BF)
                cols.append(jnp.concatenate([near, far], axis=0))
                gcols.append(jnp.where(chan == ch, ggf, 0.0).astype(BF))
            r = jnp.dot(lhs, jnp.concatenate(cols, axis=1), preferred_element_type=F32)
            q = jnp.dot(xt, jnp.concatenate(gcols, axis=1), preferred_element_type=F32)
            for k in range(2):
                ch = 2 * pair + k
                half = ch // 8
                for b in range(8):
                    piece = r[b * 16 + half * 8: b * 16 + half * 8 + 8, k * 128:(k + 1) * 128]
                    o = out[b][half]
                    out[b][half] = piece if o is None else jnp.where(sub == ch % 8, piece, o)
                n = jnp.where(lanes_i >= rows_i, q[128:, k * 128:(k + 1) * 128], q[:128, k * 128:(k + 1) * 128])
                acc = n[0:8]
                for v in range(1, 16):
                    acc = acc + pltpu.roll(n[8 * v:8 * v + 8], 128 - 8 * v, 1)
                part[ch] = acc
        for b in range(8):
            kvg_ref[rows, b * 128:(b + 1) * 128] = jnp.concatenate(out[b], axis=0).astype(BF)
        fg = part[:, 0, :]
        for u in range(1, 8):
            fg = fg + pltpu.roll(part[:, u, :], 128 - u, 1)
        fg_ref[rows, :] = fg
        return 0
    lax.fori_loop(0, 32, body, 0)

def conv_b(kv, halo, cg, after, rfilt):
    return pl.pallas_call(kernel_b, out_shape=[jax.ShapeDtypeStruct(kv.shape, BF), jax.ShapeDtypeStruct((kv.shape[0], 128), F32)],
        in_specs=[pl.BlockSpec(memory_space=pltpu.VMEM)] * 5, out_specs=[pl.BlockSpec(memory_space=pltpu.VMEM)] * 2,
        scratch_shapes=[pltpu.VMEM((16, 8, 128), F32)],
        compiler_params=pltpu.CompilerParams(vmem_limit_bytes=48 << 20))(kv, halo, cg, after, rfilt)


NCH = 2


def remote(src, dst, send, recv, **where):
    return pltpu.make_async_remote_copy(src, dst, send, recv, device_id=where, device_id_type=pl.DeviceIdType.MESH)


def exchange_kernel(
    g_ref, wt_ref, gated_ref, gate_ref, mixed_ref,
    gate_grad_ref, conv_ref, after_ref, w_grad_ref,
    gbuf, wbuf, gated_t, prod, mix, head, after,
    y1s, y1b, y2s, y2b, x1s, x1b, x2s, x2b, zs, zb,
    g_send, g_recv, s_send, s_recv, w_send, w_recv,
    y1_send, y1_recv, y2_send, y2_recv, x1_send, x1_recv, x2_send, x2_recv, z_send, z_recv,
    h_send, h_recv, l_sem, *, scale,
):
    c = lax.axis_index("ctx")
    f = lax.axis_index("fsdp")
    z, k = f // 2, f % 2
    zh, x, y = c // 16, (c // 4) % 4, c % 4
    xy = c % 16
    right, left, twin = f + 2, f - 2, f + 1 - 2 * k
    partner = (c + 16) % 32

    def at_y(d):
        return c - y + (y + d) % 4

    def at_x(d):
        return c + 4 * ((x + d) % 4 - x)

    barrier = pltpu.get_barrier_semaphore()

    def greet(**where):
        pl.semaphore_signal(barrier, inc=1, device_id=where, device_id_type=pl.DeviceIdType.MESH)

    @pl.when(z < 3)
    def _():
        greet(fsdp=right)

    @pl.when(z > 0)
    def _():
        greet(fsdp=left)

    greet(fsdp=twin)
    for d in (1, 2, 3):
        greet(ctx=at_y(d))
    greet(ctx=at_x(1))
    greet(ctx=at_x(3))
    greet(ctx=partner)

    @pl.when(c < 31)
    def _():
        greet(ctx=c + 1)

    @pl.when(c > 0)
    def _():
        greet(ctx=c - 1)

    own_g = pltpu.make_async_copy(g_ref, gbuf.at[f], l_sem.at[0])
    own_w = pltpu.make_async_copy(wt_ref, wbuf.at[xy, zh], l_sem.at[1])
    own_g.start()
    own_w.start()
    count = jnp.where(z < 3, 1, 0) + jnp.where(z > 0, 1, 0) + jnp.where(c < 31, 1, 0) + jnp.where(c > 0, 1, 0) + 7
    pl.semaphore_wait(barrier, count)
    own_g.wait()
    own_w.wait()

    span = 512 // NCH

    def g_copy(p, ch, way):
        block = gbuf.at[2 * p + k, pl.ds(ch * span, span)]
        to = right if way == 0 else left
        return remote(block, block, g_send.at[p, ch, way], g_recv.at[p, ch], fsdp=to)

    def twin_copy(p, ch):
        block = gbuf.at[2 * p + k, pl.ds(ch * span, span)]
        return remote(block, block, s_send.at[p, ch], s_recv.at[p, ch], fsdp=twin)

    def wz_copy():
        block = wbuf.at[xy, zh]
        return remote(block, block, w_send.at[0], w_recv.at[0], ctx=partner)

    def wy_copy(d):
        block = wbuf.at[xy]
        return remote(block, block, w_send.at[d], w_recv.at[d], ctx=at_y(d))

    def wx_copy(d):
        block = wbuf.at[pl.ds(4 * x, 4)]
        return remote(block, block, w_send.at[4 + d], w_recv.at[4 + d], ctx=at_x(d))

    def wf_copy(d):
        block = wbuf.at[pl.ds(4 * ((x - d) % 4) + (0 if d == 1 else 2), 2)]
        return remote(block, block, w_send.at[8 + d], w_recv.at[8 + d], ctx=at_x(d))

    wz_copy().start()
    for ch in range(NCH):
        @pl.when(z < 3)
        def _():
            g_copy(z, ch, 0).start()

        @pl.when(z > 0)
        def _():
            g_copy(z, ch, 1).start()

        twin_copy(z, ch).start()

    mix[...] = jnp.zeros_like(mix)

    def turn(i, carry):
        rows = pl.ds(pl.multiple_of(i * 128, 128), 128)
        gated_t[:, rows] = gated_ref[rows, :].astype(F32).T.astype(BF)
        return carry

    for i in range(4):
        turn(i, 0)

    wz_copy().wait_recv()
    for d in (1, 3, 2):
        wy_copy(d).start()
    for d in (1, 3, 2):
        wy_copy(d).wait_recv()
    for d in (1, 3):
        wx_copy(d).start()

    def y1_copy(b, j):
        return remote(y1s.at[b, j], y1b.at[b, j], y1_send.at[b, j], y1_recv.at[b, j], ctx=at_y(1 if j == 0 else 3))

    def y2_copy(b, j):
        return remote(y2s.at[b, j], y2b.at[b, j], y2_send.at[b, j], y2_recv.at[b, j], ctx=at_y(1 if j == 0 else 3))

    def x1_copy(b, j):
        return remote(x1s.at[b, j], x1b.at[b, j], x1_send.at[b, j], x1_recv.at[b, j], ctx=at_x(1 if j == 0 else 3))

    def x2_copy(b, j):
        return remote(x2s.at[b], x2b.at[b, j], x2_send.at[b], x2_recv.at[b, j], ctx=at_x(1 if j == 0 else 3))

    def z_copy():
        return remote(zs, zb, z_send, z_recv, ctx=partner)

    def multiply_rows(p):
        def tile(i, carry):
            b, h = 2 * p + i // 2, i % 2
            lhs = gbuf[b, pl.ds(pl.multiple_of(h * 256, 256), 256), :]
            part = jnp.dot(lhs, gated_t[...], preferred_element_type=F32)
            prod[b, pl.ds(2 * h, 2)] = part.reshape(2, 128, 512)
            return carry

        lax.fori_loop(0, 4, tile, 0)
        for i in range(2):
            b = 2 * p + i
            far = prod[b, (y + 2) % 4].astype(BF)
            y1s[b, 0] = far[:, :256]
            y1s[b, 1] = far[:, 256:]
            for j in range(2):
                y1_copy(b, j).start()

    def multiply_columns(p):
        def tile(i, carry):
            b, h, n = 2 * p + i // 4, (i // 2) % 2, i % 2
            rows = pl.ds(pl.multiple_of(h * 256, 256), 256)
            cols = pl.ds(pl.multiple_of(n * 512, 512), 512)
            lhs = jnp.concatenate([wbuf[4 * (b % 4) + q, b // 4, rows, :] for q in range(4)], axis=1)
            mix[rows, cols] += jnp.dot(lhs, gbuf[b, :, cols], preferred_element_type=F32)
            return carry

        lax.fori_loop(0, 8, tile, 0)

    def round_y2(p):
        for i in range(2):
            b = 2 * p + i
            y1_copy(b, 0).wait_recv()
            up = prod[b, (y + 1) % 4]
            y2s[b, 0, :, :256] = (up[:, :256] + y1b[b, 0].astype(F32)).astype(BF)
            y2s[b, 0, :, 256:] = up[:, 256:].astype(BF)
            y2_copy(b, 0).start()
            y1_copy(b, 1).wait_recv()
            down = prod[b, (y + 3) % 4]
            y2s[b, 1, :, :256] = down[:, :256].astype(BF)
            y2s[b, 1, :, 256:] = (down[:, 256:] + y1b[b, 1].astype(F32)).astype(BF)
            y2_copy(b, 1).start()

    def round_x1(p):
        for i in range(2):
            b = 2 * p + i
            y2_copy(b, 0).wait_recv()
            y2_copy(b, 1).wait_recv()
            total = prod[b, y] + y2b[b, 0].astype(F32) + y2b[b, 1].astype(F32)
            prod[b, y] = total

            @pl.when((x - b) % 4 == 2)
            def _():
                x1s[b, 0] = total[:, :256].astype(BF)
                x1s[b, 1] = total[:, 256:].astype(BF)
                for j in range(2):
                    x1_copy(b, j).start()

    def round_x2(p):
        for i in range(2):
            b = 2 * p + i
            role = (x - b) % 4

            @pl.when(role == 3)
            def _():
                x1_copy(b, 0).wait_recv()
                x2s[b, :, :256] = (prod[b, y, :, :256] + x1b[b, 0].astype(F32)).astype(BF)
                x2s[b, :, 256:] = prod[b, y, :, 256:].astype(BF)
                x2_copy(b, 0).start()

            @pl.when(role == 1)
            def _():
                x1_copy(b, 1).wait_recv()
                x2s[b, :, :256] = prod[b, y, :, :256].astype(BF)
                x2s[b, :, 256:] = (prod[b, y, :, 256:] + x1b[b, 1].astype(F32)).astype(BF)
                x2_copy(b, 1).start()

    def round_z(p):
        for i in range(2):
            b = 2 * p + i

            @pl.when((x - b) % 4 == 0)
            def _():
                x2_copy(b, 0).wait_recv()
                x2_copy(b, 1).wait_recv()
                total = prod[b, y] + x2b[b, 0].astype(F32) + x2b[b, 1].astype(F32)

                @pl.when(b // 4 == zh)
                def _():
                    prod[b, y] = total

                @pl.when(b // 4 != zh)
                def _():
                    zs[...] = total.astype(BF)
                    z_copy().start()

    def sides(s, act):
        @pl.when(z >= s)
        def _():
            act(z - s)

        @pl.when((s > 0) & (z + s < 4))
        def _():
            act(z + s)

    def step(s, carry):
        for ch in range(NCH):
            @pl.when((s > 0) & (z >= s))
            def _():
                g_copy(z - s, ch, 0).wait_recv()

                @pl.when(z < 3)
                def _():
                    g_copy(z - s, ch, 0).start()

                twin_copy(z - s, ch).start()

            @pl.when((s > 0) & (z + s < 4))
            def _():
                g_copy(z + s, ch, 1).wait_recv()

                @pl.when(z > 0)
                def _():
                    g_copy(z + s, ch, 1).start()

                twin_copy(z + s, ch).start()

        def arrive(p):
            for ch in range(NCH):
                twin_copy(p, ch).wait_recv()
            multiply_rows(p)

        sides(s, arrive)

        @pl.when(s > 0)
        def _():
            sides(s - 1, round_x2)

        @pl.when(s == 1)
        def _():
            wx_copy(1).wait_recv()
            wf_copy(1).start()
            wx_copy(3).wait_recv()
            wf_copy(3).start()

        @pl.when(s == 2)
        def _():
            wf_copy(1).wait_recv()
            wf_copy(3).wait_recv()

        @pl.when(s >= 2)
        def _():
            def late(q, carry):
                sides(q, multiply_columns)
                return carry

            lax.fori_loop(jnp.where(s == 2, 0, 3), s + 1, late, 0)

        sides(s, round_y2)

        @pl.when(s > 0)
        def _():
            sides(s - 1, round_z)

        sides(s, round_x1)
        return carry

    lax.fori_loop(0, 4, step, 0)

    def finish(i, carry):
        rows = pl.ds(pl.multiple_of(i * 32, 32), 32)
        wide = mix[rows, :]
        gate_grad_ref[rows, :] = wide * mixed_ref[rows, :].astype(F32)
        conv = (wide * gate_ref[rows, :].astype(F32)).astype(BF)
        conv_ref[rows, :] = conv
        head[rows, :] = conv[:, :128]
        return carry

    lax.fori_loop(0, 16, finish, 0)

    def h_copy():
        return remote(head, after, h_send, h_recv, ctx=c - 1)

    @pl.when(c > 0)
    def _():
        h_copy().start()

    sides(3, round_x2)
    sides(3, round_z)

    @pl.when(c < 31)
    def _():
        h_copy().wait_recv()
        after_ref[...] = after[...]

    @pl.when(c == 31)
    def _():
        after_ref[...] = jnp.zeros_like(after_ref)

    z_copy().wait_recv()
    w_grad_ref[...] = (prod[4 * zh + x, y] + zb[...].astype(F32)) * scale

    def sent_blocks(p, carry):
        for ch in range(NCH):
            @pl.when((p <= z) & (z < 3))
            def _():
                g_copy(p, ch, 0).wait_send()

            @pl.when((p >= z) & (z > 0))
            def _():
                g_copy(p, ch, 1).wait_send()

            twin_copy(p, ch).wait_send()
        return carry

    lax.fori_loop(0, 4, sent_blocks, 0)

    def sent_sums(b, carry):
        for j in range(2):
            y1_copy(b, j).wait_send()
            y2_copy(b, j).wait_send()
        role = (x - b) % 4

        @pl.when(role == 2)
        def _():
            for j in range(2):
                x1_copy(b, j).wait_send()

        @pl.when(role % 2 == 1)
        def _():
            x2_copy(b, 0).wait_send()

        return carry

    lax.fori_loop(0, 8, sent_sums, 0)
    z_copy().wait_send()
    wz_copy().wait_send()
    for d in (1, 2, 3):
        wy_copy(d).wait_send()
    for d in (1, 3):
        wx_copy(d).wait_send()
        wf_copy(d).wait_send()

    @pl.when(c > 0)
    def _():
        h_copy().wait_send()


def exchange(out_grad, wt, gated, gate, mixed, scale):
    vmem = pl.BlockSpec(memory_space=pltpu.VMEM)
    dma = pltpu.SemaphoreType.DMA
    return pl.pallas_call(
        functools.partial(exchange_kernel, scale=scale),
        out_shape=[
            jax.ShapeDtypeStruct((512, 1024), F32),
            jax.ShapeDtypeStruct((512, 1024), BF),
            jax.ShapeDtypeStruct((512, 128), BF),
            jax.ShapeDtypeStruct((128, 512), F32),
        ],
        in_specs=[vmem] * 5,
        out_specs=[vmem] * 4,
        scratch_shapes=[
            pltpu.VMEM((8, 512, 1024), BF),
            pltpu.VMEM((16, 2, 512, 128), BF),
            pltpu.VMEM((1024, 512), BF),
            pltpu.VMEM((8, 4, 128, 512), F32),
            pltpu.VMEM((512, 1024), F32),
            pltpu.VMEM((512, 128), BF),
            pltpu.VMEM((512, 128), BF),
            pltpu.VMEM((8, 2, 128, 256), BF),
            pltpu.VMEM((8, 2, 128, 256), BF),
            pltpu.VMEM((8, 2, 128, 512), BF),
            pltpu.VMEM((8, 2, 128, 512), BF),
            pltpu.VMEM((8, 2, 128, 256), BF),
            pltpu.VMEM((8, 2, 128, 256), BF),
            pltpu.VMEM((8, 128, 512), BF),
            pltpu.VMEM((8, 2, 128, 512), BF),
            pltpu.VMEM((128, 512), BF),
            pltpu.VMEM((128, 512), BF),
            dma((4, NCH, 2)), dma((4, NCH)), dma((4, NCH)), dma((4, NCH)), dma((12,)), dma((12,)),
            dma((8, 2)), dma((8, 2)), dma((8, 2)), dma((8, 2)), dma((8, 2)), dma((8, 2)), dma((8,)), dma((8, 2)),
            dma, dma, dma, dma, dma((2,)),
        ],
        compiler_params=pltpu.CompilerParams(
            collective_id=0, has_side_effects=True, vmem_limit_bytes=60 << 20
        ),
    )(out_grad, wt, gated, gate, mixed)


def on_device(out_grad, gate_values, kv_product, w_out, filters):
    ctx_count = lax.axis_size("ctx")
    norm_scale = 1.0 / math.sqrt(ctx_count * out_grad.shape[1])
    own_filters = filters.reshape(filters.shape[2:])
    taps = lax.all_gather(own_filters, "ctx", axis=0, tiled=True)
    before = lax.ppermute(kv_product[:, -128:], "ctx", [(i, i + 1) for i in range(ctx_count - 1)])
    mixed, gated = conv_a(kv_product, before, gate_values, taps)
    gate_grad, conv_grad, after, w_grad = exchange(out_grad, w_out.T, gated, gate_values, mixed, norm_scale)
    turned = jnp.roll(taps[:, ::-1], 1, axis=1)
    kv_grad, filter_part = conv_b(kv_product, before, conv_grad, after, turned)
    filter_grad = lax.psum_scatter(filter_part, "ctx", scatter_dimension=0, tiled=True) * norm_scale
    return (gate_grad, kv_grad, filter_grad.reshape(filters.shape), w_grad)


def solution(mesh):
    in_specs = (
        P("fsdp", "ctx"),
        P("fsdp", "ctx"),
        P("fsdp", "ctx"),
        P("ctx", "fsdp"),
        P("fsdp", "ctx", None, None),
    )
    out_specs = (P("fsdp", "ctx"), P("fsdp", "ctx"), P("fsdp", "ctx", None, None), P("ctx", "fsdp"))
    return jax.shard_map(
        on_device, mesh=mesh, in_specs=in_specs, out_specs=out_specs, check_vma=False
    )
```

time: 577 us -> 531 us (0.920)
  Pallas kernels: 0 us -> 134 us
  waiting for transfers between devices: 376 us -> 251 us
  local copies, waits for them, and re-layouts: 49.6 us -> 10.5 us
  blocking collectives: 90.8 us -> 116 us
  matrix products: 23.3 us -> 0 us
  starting transfers between devices: 18.4 us -> 3.53 us
    all_gather x2 -> x0, waiting for transfers between devices: 138 us -> none  [the longest x1 86.7 us: on_device(): grad_full = lax.all_gather(out_grad, 'fsdp', axis=0, tiled=True)]
    pallas_call x0 -> x3, Pallas kernels: none -> 134 us  [the longest x1 92.3 us: exchange(): pl.pallas_call(functools.partial(exchange_kernel, scale=scale), out_shape...]
    all_gather x0 -> x1, blocking collectives: none -> 116 us  [on_device(): taps = lax.all_gather(own_filters, 'ctx', axis=0, tiled=True)]
    all_to_all x2 -> x0, blocking collectives: 90.8 us -> none  [the longest x1 59.1 us: on_device(): lax.all_to_all(conv_grad, 'ctx', split_axis=0, concat_axis=1, tiled=True)]
    reduce_scatter x1, waiting for transfers between devices: 210 us -> 251 us  [on_device(): lax.psum_scatter(filter_part, 'ctx', scatter_dimension=0, tiled=True)]
    all_to_all x2 -> x0, waiting for transfers between devices: 26.4 us -> none  [the longest x1 23.4 us: on_device(): lax.all_to_all(kv_product, 'ctx', split_axis=0, concat_axis=1, tiled=True)]
    dot_general x8 -> x0, matrix products: 23.3 us -> none  [the longest x1 11.6 us: on_device(): lax.dot_general(lax.all_gather(w_out, 'ctx', axis=0, tiled=True), grad_pa...]
    reshape x8 -> x0, local copies, waits for them, and re-layouts: 22.4 us -> none  [the longest x4 14.7 us: make_band(): window_cut.reshape(channels, tap_count, 2 * tap_count - 1)[:, :, :tap_count]]
  transfers between devices with their start and end apart: 5 -> 2, of which waited for: 5 -> 1; matrix products, arithmetic and copies ran while one was open for 9% -> 0% of each run, Pallas kernels for 0% -> 0%
where the time goes in v1:
time: 531 us
  waiting for transfers between devices  251 us (47%)
  Pallas kernels  134 us (25%)
  blocking collectives  116 us (22%)
  between operations  14.1 us (3%)
  local copies, waits for them, and re-layouts  10.5 us (2%)
    reduce_scatter x1, waiting for transfers between devices, on_device(): lax.psum_scatter(filter_part, 'ctx', scatter_dimension=0, tiled=True)  251 us
    all_gather x1, blocking collectives, on_device(): taps = lax.all_gather(own_filters, 'ctx', axis=0, tiled=True)  116 us
    pallas_call x1, Pallas kernels, exchange(): pl.pallas_call(functools.partial(exchange_kernel, scale=scale), out_shape...  92.3 us
    pallas_call x1, Pallas kernels, conv_b(): pl.pallas_call(kernel_b, out_shape=[jax.ShapeDtypeStruct(kv.shape, BF), j...  28.1 us
    pallas_call x1, Pallas kernels, conv_a(): pl.pallas_call(kernel_a, out_shape=[jax.ShapeDtypeStruct(kv.shape, BF)] *...  13.2 us
  transfers between devices with their start and end apart: 2, of which 1 were waited for; matrix products, arithmetic and copies ran while one was open for 0% of the time, Pallas kernels for 0%

profile of v1, /device:TPU:32, one launch (start us, length us, event | category | flops | bytes accessed | tf_op | source)
XLA Modules:
  0.0 530.7 jit_solution(7449754197110543047)
XLA Ops:
  7.2 0.0 copy-start
  7.2 0.0 reduce-scatter.2.cloned.1.call-start
  7.2 1.0 slice.15
  8.2 3.5 collective-permute-start
  11.7 116.2 %all-gather = bf16[1,1,512,128]{3,2,1,0:T(8,128)(2,1)S(1)} all-gather(bf16[1,1,16,128]{3,2,1,0:T(8,128)(2,1)} %param.9), channel_id=2, replica_groups=mesh['ctx'=32,'fsdp'=8] {'ctx'}, dimensions={2}, use_global_device_ids=true | all-gather | bytes 135168 | tf_op jit(solution)/shard_map/all_gather | solution.py:544
  127.9 1.7 copy.9
  129.5 0.1 slice.20
  129.6 0.4 slice.18
  130.0 0.1 pad_maximum_fusion.rfilt_ref
  130.2 0.0 collective-permute-done.halo_ref
  130.2 0.0 copy-done
  130.2 0.0 copy-start.1
  130.2 1.2 copy-done.1
  131.4 13.2 %shard_map.84 = (bf16[512,1024]{1,0:T(8,128)(2,1)S(1)}, bf16[512,1024]{1,0:T(8,128)(2,1)S(1)}) custom-call(bf16[512,1024]{1,0:T(8,128)(2,1)S(1)} %copy-done, bf16[512,128]{1,0:T(8,128)(2,1)S(1)} %collective-permute-done.halo_ref, bf16[512,1024]{1,0:T(8,128)(2,1)S(1)} %copy-done.1, bf16[512,128]{1,0:T(8,128)(2,1)S(1)} %bitcast.7), custom_call_target="tpu_custom_call" | custom-call | tf_op jit(solution)/shard_map/pallas_call | solution.py:55
  144.6 0.0 copy-start.3
  144.6 1.0 copy-done.3
  145.6 0.0 copy-start.4
  145.6 1.0 copy-done.4
  146.6 92.3 %shard_map.85 = (f32[512,1024]{1,0:T(8,128)}, bf16[512,1024]{1,0:T(8,128)(2,1)}, bf16[512,128]{1,0:T(8,128)(2,1)}, f32[128,512]{1,0:T(8,128)}) custom-call(bf16[512,1024]{1,0:T(8,128)(2,1)} %g_ref.1, bf16[512,128]{1,0:T(8,128)(2,1)} %bitcast.8, bf16[512,1024]{1,0:T(8,128)(2,1)} %copy-done.4, bf16[512,1024]{1,0:T(8,128)(2,1)} %gate_ref.3, ...), custom_call_target="tpu_custom_call" | custom-call | tf_op jit(solution)/shard_map/pallas_call | solution.py:502
  238.9 0.0 copy-start.2
  238.9 1.2 copy-done.2
  240.1 0.0 copy-start.5
  240.1 0.9 copy-done.5
  241.0 0.0 copy-start.6
  241.0 28.1 %shard_map.86 = (bf16[512,1024]{1,0:T(8,128)(2,1)}, f32[512,128]{1,0:T(8,128)}) custom-call(bf16[512,1024]{1,0:T(8,128)(2,1)S(1)} %copy-done, bf16[512,128]{1,0:T(8,128)(2,1)S(1)} %collective-permute-done.halo_ref, bf16[512,1024]{1,0:T(8,128)(2,1)S(1)} %copy-done.2, bf16[512,128]{1,0:T(8,128)(2,1)S(1)} %copy-done.5, ...), custom_call_target="tpu_custom_call" | custom-call | tf_op jit(solution)/shard_map/pallas_call | solution.py:107
  269.1 0.0 reduce-scatter.2.cloned.1.call-update
  269.2 251.4 %reduce-scatter.2.cloned.1.call-done = f32[16,128]{1,0:T(8,128)} async-done(((f32[512,128]{1,0:T(8,128)}), f32[16,128]{1,0:T(8,128)}) %reduce-scatter.2.cloned.1.call-update) | async-done | bytes 8208 | tf_op jit(solution)/shard_map/reduce_scatter | solution.py:550
  520.5 1.3 multiply_bitcast_fusion
  521.8 0.0 copy-done.6
  521.8 1.3 copy.12
  523.2 0.0 copy-done.7
  523.2 0.7 copy.13
  (1 shorter events, 0.0 us)
Async XLA Ops:
  7.2 123.0 %copy-start = (bf16[512,1024]{1,0:T(8,128)(2,1)S(1)}, bf16[512,1024]{1,0:T(8,128)(2,1)}, u32[]{:S(2)}) copy-start(bf16[512,1024]{1,0:T(8,128)(2,1)} %kv_ref.3) | copy-start | bytes 3145732
  7.2 513.4 %reduce-scatter.2.cloned.1.call-start = ((), (), s32[]{:S(2)}) async-start(), calls=%async_computation.1 | async-start | bytes 270336 | tf_op jit(solution)/shard_map/reduce_scatter | solution.py:550
  8.2 121.9 %collective-permute-start = (bf16[512,128]{1,0:T(8,128)(2,1)S(1)}, bf16[512,128]{1,0:T(8,128)(2,1)S(1)}, u32[]{:S(2)}, u32[]{:S(2)}) collective-permute-start(bf16[512,128]{1,0:T(8,128)(2,1)S(1)} %slice.15), channel_id=1, source_target_pairs={{0,8},{8,16},{16,24},{24,32},{32,40},{40,48},{48,56},{56,64},{64,7... | collective-permute-start | bytes 393224 | tf_op jit(solution)/shard_map/ppermute | solution.py:545
  130.2 1.2 copy-start.1
  144.6 1.0 copy-start.3
  145.6 1.0 copy-start.4
  238.9 1.2 copy-start.2
  240.1 0.9 copy-start.5
  241.0 280.9 %copy-start.6 = (f32[512,1024]{1,0:T(8,128)S(1)}, f32[512,1024]{1,0:T(8,128)}, u32[]{:S(2)}) copy-start(f32[512,1024]{1,0:T(8,128)} %get-tuple-element.24) | copy-start | bytes 6291460
  521.8 1.3 copy-start.7
Sparse Core Ops, SparseCore 0:
  269.3 251.2 reduce-scatter.1

commit v2 on v1

--- a/solution.py
+++ b/solution.py
@@ -11,7 +11,8 @@
 F32 = jnp.float32
 BF = jnp.bfloat16
 
-def band_pair(row):
+
+def bands(row):
     rows = lax.broadcasted_iota(jnp.int32, (128, 128), 0)
     lanes = lax.broadcasted_iota(jnp.int32, (128, 128), 1)
     turned = pltpu.roll(jnp.broadcast_to(row, (128, 128)), 0, 1, stride=1, stride_axis=0)
@@ -19,95 +20,65 @@
     far = jnp.where(lanes < rows, turned, 0.0).astype(BF)
     return far, near
 
-def conv_group(h16, lhs, swap):
+
+def stack_blocks(parts):
+    return jnp.concatenate(
+        [jnp.concatenate([parts[b], parts[b + 1]], axis=1) for b in range(8)], axis=0
+    )
+
+
+def keep_own(out, product, ch, column):
     sub = lax.broadcasted_iota(jnp.int32, (8, 128), 0)
+    half = ch // 8
+    for b in range(8):
+        start = b * 16 + half * 8
+        piece = product[start : start + 8, column * 128 : (column + 1) * 128]
+        old = out[b][half]
+        out[b][half] = piece if old is None else jnp.where(sub == ch % 8, piece, old)
+
+
+def conv_group(taps, lhs, _):
     out = [[None, None] for _ in range(8)]
     for pair in range(8):
-        cols = []
+        cols = [jnp.concatenate(bands(taps[ch : ch + 1, :]), axis=0) for ch in (2 * pair, 2 * pair + 1)]
+        product = jnp.dot(lhs, jnp.concatenate(cols, axis=1), preferred_element_type=F32)
+        for i in range(2):
+            keep_own(out, product, 2 * pair + i, i)
+    return [jnp.concatenate(o, axis=0) for o in out]
+
+
+def back_group(before, kv, grad, after, rows, taps, part):
+    xs = [before[rows, :]] + [kv[rows, b * 128 : (b + 1) * 128] for b in range(8)]
+    gs = [grad[rows, b * 128 : (b + 1) * 128] for b in range(8)] + [after[rows, :]]
+    row_at = lax.broadcasted_iota(jnp.int32, (128, 128), 0)
+    lane_at = lax.broadcasted_iota(jnp.int32, (128, 128), 1)
+    lhs = stack_blocks(gs)
+    x_turned = stack_blocks(xs).astype(F32).T.astype(BF)
+    wide = jnp.concatenate(gs[:8], axis=0).astype(F32)
+    out = [[None, None] for _ in range(8)]
+    for pair in range(8):
+        band_rows, own_grad = [], []
         for ch in (2 * pair, 2 * pair + 1):
-            far, near = band_pair(h16[ch:ch + 1, :])
-            cols.append(jnp.concatenate([far, near] if not swap else [near, far], axis=0))
-        w = jnp.concatenate(cols, axis=1)
-        r = jnp.dot(lhs, w, preferred_element_type=F32)
-        for k in range(2):
-            ch = 2 * pair + k
-            half = ch // 8
-            for b in range(8):
-                piece = r[b * 16 + half * 8: b * 16 + half * 8 + 8, k * 128:(k + 1) * 128]
-                o = out[b][half]
-                out[b][half] = piece if o is None else jnp.where(sub == ch % 8, piece, o)
-    return [jnp.concatenate(o, axis=0) for o in out]
-
-def kernel_a(kv_ref, halo_ref, gate_ref, filt_ref, mixed_ref, gated_ref):
-    def body(g, _):
-        rows = pl.ds(pl.multiple_of(g * 16, 16), 16)
-        xs = [halo_ref[rows, :]] + [kv_ref[rows, b * 128:(b + 1) * 128] for b in range(8)]
-        lhs = jnp.concatenate([jnp.concatenate([xs[b], xs[b + 1]], axis=1) for b in range(8)], axis=0)
-        outs = conv_group(filt_ref[rows, :].astype(F32), lhs, False)
-        for b in range(8):
-            m = outs[b].astype(BF)
-            mixed_ref[rows, b * 128:(b + 1) * 128] = m
-            gated_ref[rows, b * 128:(b + 1) * 128] = (gate_ref[rows, b * 128:(b + 1) * 128].astype(F32) * m.astype(F32)).astype(BF)
-        return 0
-    lax.fori_loop(0, 32, body, 0)
-
-def conv_a(kv, halo, gate, filt):
-    return pl.pallas_call(kernel_a, out_shape=[jax.ShapeDtypeStruct(kv.shape, BF)] * 2,
-        in_specs=[pl.BlockSpec(memory_space=pltpu.VMEM)] * 4, out_specs=[pl.BlockSpec(memory_space=pltpu.VMEM)] * 2,
-        compiler_params=pltpu.CompilerParams(vmem_limit_bytes=48 << 20))(kv, halo, gate, filt)
-
-def kernel_b(kv_ref, halo_ref, cg_ref, after_ref, rfilt_ref, kvg_ref, fg_ref, part):
-    rows_i = lax.broadcasted_iota(jnp.int32, (128, 128), 0)
-    lanes_i = lax.broadcasted_iota(jnp.int32, (128, 128), 1)
-    def body(g, _):
-        rows = pl.ds(pl.multiple_of(g * 16, 16), 16)
-        xs = [halo_ref[rows, :]] + [kv_ref[rows, b * 128:(b + 1) * 128] for b in range(8)]
-        gs = [cg_ref[rows, b * 128:(b + 1) * 128] for b in range(8)] + [after_ref[rows, :]]
-        lhs = jnp.concatenate([jnp.concatenate([gs[b], gs[b + 1]], axis=1) for b in range(8)], axis=0)
-        hr = rfilt_ref[rows, :].astype(F32)
-        sub = lax.broadcasted_iota(jnp.int32, (8, 128), 0)
-        out = [[None, None] for _ in range(8)]
-        x = jnp.concatenate([jnp.concatenate([xs[b], xs[b + 1]], axis=1) for b in range(8)], axis=0)
-        xt = x.astype(F32).T.astype(BF)
-        gg = jnp.concatenate(gs[:8], axis=0)
-        chan = lax.broadcasted_iota(jnp.int32, (128, 128), 0) % 16
-        ggf = gg.astype(F32)
-        for pair in range(8):
-            cols = []; gcols = []
-            for ch in (2 * pair, 2 * pair + 1):
-                turned = pltpu.roll(jnp.broadcast_to(hr[ch:ch + 1, :], (128, 128)), 0, 1, stride=1, stride_axis=0)
-                near = jnp.where(rows_i >= lanes_i, turned, 0.0).astype(BF)
-                far = jnp.where(rows_i < lanes_i, turned, 0.0).astype(BF)
-                cols.append(jnp.concatenate([near, far], axis=0))
-                gcols.append(jnp.where(chan == ch, ggf, 0.0).astype(BF))
-            r = jnp.dot(lhs, jnp.concatenate(cols, axis=1), preferred_element_type=F32)
-            q = jnp.dot(xt, jnp.concatenate(gcols, axis=1), preferred_element_type=F32)
-            for k in range(2):
-                ch = 2 * pair + k
-                half = ch // 8
-                for b in range(8):
-                    piece = r[b * 16 + half * 8: b * 16 + half * 8 + 8, k * 128:(k + 1) * 128]
-                    o = out[b][half]
-                    out[b][half] = piece if o is None else jnp.where(sub == ch % 8, piece, o)
-                n = jnp.where(lanes_i >= rows_i, q[128:, k * 128:(k + 1) * 128], q[:128, k * 128:(k + 1) * 128])
-                acc = n[0:8]
-                for v in range(1, 16):
-                    acc = acc + pltpu.roll(n[8 * v:8 * v + 8], 128 - 8 * v, 1)
-                part[ch] = acc
-        for b in range(8):
-            kvg_ref[rows, b * 128:(b + 1) * 128] = jnp.concatenate(out[b], axis=0).astype(BF)
-        fg = part[:, 0, :]
-        for u in range(1, 8):
-            fg = fg + pltpu.roll(part[:, u, :], 128 - u, 1)
-        fg_ref[rows, :] = fg
-        return 0
-    lax.fori_loop(0, 32, body, 0)
-
-def conv_b(kv, halo, cg, after, rfilt):
-    return pl.pallas_call(kernel_b, out_shape=[jax.ShapeDtypeStruct(kv.shape, BF), jax.ShapeDtypeStruct((kv.shape[0], 128), F32)],
-        in_specs=[pl.BlockSpec(memory_space=pltpu.VMEM)] * 5, out_specs=[pl.BlockSpec(memory_space=pltpu.VMEM)] * 2,
-        scratch_shapes=[pltpu.VMEM((16, 8, 128), F32)],
-        compiler_params=pltpu.CompilerParams(vmem_limit_bytes=48 << 20))(kv, halo, cg, after, rfilt)
+            far, near = bands(taps[ch : ch + 1, :])
+            band_rows.append(jnp.concatenate([near, far], axis=1))
+            own_grad.append(jnp.where(row_at % 16 == ch, wide, 0.0).astype(BF))
+        product = lax.dot_general(
+            lhs, jnp.concatenate(band_rows, axis=0), (((1,), (1,)), ((), ())), preferred_element_type=F32
+        )
+        outer = jnp.dot(x_turned, jnp.concatenate(own_grad, axis=1), preferred_element_type=F32)
+        for i in range(2):
+            ch = 2 * pair + i
+            keep_own(out, product, ch, i)
+            cols = slice(i * 128, (i + 1) * 128)
+            both = jnp.where(lane_at >= row_at, outer[128:, cols], outer[:128, cols])
+            acc = both[0:8]
+            for v in range(1, 16):
+                acc = acc + pltpu.roll(both[8 * v : 8 * v + 8], 128 - 8 * v, 1)
+            part[ch] = acc
+    taps_part = part[:, 0, :]
+    for u in range(1, 8):
+        taps_part = taps_part + pltpu.roll(part[:, u, :], 128 - u, 1)
+    return [jnp.concatenate(o, axis=0) for o in out], taps_part
 
 
 NCH = 2
@@ -118,13 +89,14 @@
 
 
 def exchange_kernel(
-    g_ref, wt_ref, gated_ref, gate_ref, mixed_ref,
-    gate_grad_ref, conv_ref, after_ref, w_grad_ref,
-    gbuf, wbuf, gated_t, prod, mix, head, after,
+    g_ref, w_ref, gate_hbm, kv_hbm, filt_ref,
+    gate_grad_ref, kv_grad_ref, filt_grad_ref, w_grad_ref,
+    gbuf, wbuf, gated_t, prod, mix, head, after, tail, before, taps,
+    gate, kv, mixed, work, part, fsum, fy, fx, fz, fxs, fzs,
     y1s, y1b, y2s, y2b, x1s, x1b, x2s, x2b, zs, zb,
     g_send, g_recv, s_send, s_recv, w_send, w_recv,
     y1_send, y1_recv, y2_send, y2_recv, x1_send, x1_recv, x2_send, x2_recv, z_send, z_recv,
-    h_send, h_recv, l_sem, *, scale,
+    h_send, h_recv, b_send, b_recv, t_send, t_recv, f_send, f_recv, l_sem, *, scale,
 ):
     c = lax.axis_index("ctx")
     f = lax.axis_index("fsdp")
@@ -156,8 +128,8 @@
     greet(fsdp=twin)
     for d in (1, 2, 3):
         greet(ctx=at_y(d))
-    greet(ctx=at_x(1))
-    greet(ctx=at_x(3))
+    for d in (1, 2, 3):
+        greet(ctx=at_x(d))
     greet(ctx=partner)
 
     @pl.when(c < 31)
@@ -169,13 +141,27 @@
         greet(ctx=c - 1)
 
     own_g = pltpu.make_async_copy(g_ref, gbuf.at[f], l_sem.at[0])
-    own_w = pltpu.make_async_copy(wt_ref, wbuf.at[xy, zh], l_sem.at[1])
+    own_kv = pltpu.make_async_copy(kv_hbm, kv, l_sem.at[1])
+    own_gate = pltpu.make_async_copy(gate_hbm, gate, l_sem.at[2])
+    own_kv.start()
     own_g.start()
-    own_w.start()
-    count = jnp.where(z < 3, 1, 0) + jnp.where(z > 0, 1, 0) + jnp.where(c < 31, 1, 0) + jnp.where(c > 0, 1, 0) + 7
+    own_gate.start()
+    wbuf[xy, zh] = w_ref[...].astype(F32).T.astype(BF)
+    taps[xy, zh] = filt_ref[...]
+    own_kv.wait()
+    tail[...] = kv[:, 896:]
+
+    @pl.when(c == 0)
+    def _():
+        before[...] = jnp.zeros_like(before)
+
+    @pl.when(c == 31)
+    def _():
+        after[...] = jnp.zeros_like(after)
+
+    count = jnp.where(z < 3, 1, 0) + jnp.where(z > 0, 1, 0) + jnp.where(c < 31, 1, 0) + jnp.where(c > 0, 1, 0) + 8
     pl.semaphore_wait(barrier, count)
     own_g.wait()
-    own_w.wait()
 
     span = 512 // NCH
 
@@ -204,6 +190,27 @@
         block = wbuf.at[pl.ds(4 * ((x - d) % 4) + (0 if d == 1 else 2), 2)]
         return remote(block, block, w_send.at[8 + d], w_recv.at[8 + d], ctx=at_x(d))
 
+    def b_copy():
+        return remote(tail, before, b_send, b_recv, ctx=c + 1)
+
+    def tz_copy():
+        block = taps.at[xy, zh]
+        return remote(block, block, t_send.at[0], t_recv.at[0], ctx=partner)
+
+    def ty_copy(d):
+        block = taps.at[xy]
+        return remote(block, block, t_send.at[d], t_recv.at[d], ctx=at_y(d))
+
+    def tx_copy(d):
+        block = taps.at[pl.ds(4 * x, 4)]
+        return remote(block, block, t_send.at[4 + d], t_recv.at[4 + d], ctx=at_x(d))
+
+    tz_copy().start()
+
+    @pl.when(c < 31)
+    def _():
+        b_copy().start()
+
     wz_copy().start()
     for ch in range(NCH):
         @pl.when(z < 3)
@@ -218,21 +225,51 @@
 
     mix[...] = jnp.zeros_like(mix)
 
-    def turn(i, carry):
-        rows = pl.ds(pl.multiple_of(i * 128, 128), 128)
-        gated_t[:, rows] = gated_ref[rows, :].astype(F32).T.astype(BF)
-        return carry
-
-    for i in range(4):
-        turn(i, 0)
-
+    tz_copy().wait_recv()
+    for d in (1, 3, 2):
+        ty_copy(d).start()
+    for d in (1, 3, 2):
+        ty_copy(d).wait_recv()
+    for d in (1, 3, 2):
+        tx_copy(d).start()
     wz_copy().wait_recv()
     for d in (1, 3, 2):
         wy_copy(d).start()
     for d in (1, 3, 2):
+        tx_copy(d).wait_recv()
+
+    @pl.when(c > 0)
+    def _():
+        b_copy_in = b_copy()
+        b_copy_in.wait_recv()
+
+    own_gate.wait()
+
+    def filter_forward(g, carry):
+        rows = pl.ds(pl.multiple_of(g * 16, 16), 16)
+        xs = [before[rows, :]] + [kv[rows, b * 128 : (b + 1) * 128] for b in range(8)]
+        lhs = jnp.concatenate([jnp.concatenate([xs[b], xs[b + 1]], axis=1) for b in range(8)], axis=0)
+        outs = conv_group(taps[g % 16, g // 16].astype(F32), lhs, False)
+        for b in range(8):
+            cols = slice(b * 128, (b + 1) * 128)
+            narrow = outs[b].astype(BF)
+            mixed[rows, cols] = narrow
+            work[rows, cols] = (gate[rows, cols].astype(F32) * narrow.astype(F32)).astype(BF)
+        return carry
+
+    lax.fori_loop(0, 16, filter_forward, 0)
+    for d in (1, 3, 2):
         wy_copy(d).wait_recv()
     for d in (1, 3):
         wx_copy(d).start()
+    lax.fori_loop(16, 32, filter_forward, 0)
+
+    def turn(i, carry):
+        cols = pl.ds(pl.multiple_of(i * 128, 128), 128)
+        gated_t[:, cols] = work[cols, :].astype(F32).T.astype(BF)
+        return carry
+
+    lax.fori_loop(0, 4, turn, 0)
 
     def y1_copy(b, j):
         return remote(y1s.at[b, j], y1b.at[b, j], y1_send.at[b, j], y1_recv.at[b, j], ctx=at_y(1 if j == 0 else 3))
@@ -417,38 +454,78 @@
 
     lax.fori_loop(0, 4, step, 0)
 
+    def h_copy():
+        return remote(head, after, h_send, h_recv, ctx=c - 1)
+
+    def finish_head(i, carry):
+        rows = pl.ds(pl.multiple_of(i * 64, 64), 64)
+        head[rows, :] = (mix[rows, :128] * gate[rows, :128].astype(F32)).astype(BF)
+        return carry
+
+    lax.fori_loop(0, 8, finish_head, 0)
+
+    @pl.when(c > 0)
+    def _():
+        h_copy().start()
+
     def finish(i, carry):
         rows = pl.ds(pl.multiple_of(i * 32, 32), 32)
         wide = mix[rows, :]
-        gate_grad_ref[rows, :] = wide * mixed_ref[rows, :].astype(F32)
-        conv = (wide * gate_ref[rows, :].astype(F32)).astype(BF)
-        conv_ref[rows, :] = conv
-        head[rows, :] = conv[:, :128]
+        work[rows, :] = (wide * gate[rows, :].astype(F32)).astype(BF)
+        mix[rows, :] = wide * mixed[rows, :].astype(F32)
         return carry
 
     lax.fori_loop(0, 16, finish, 0)
-
-    def h_copy():
-        return remote(head, after, h_send, h_recv, ctx=c - 1)
-
-    @pl.when(c > 0)
-    def _():
-        h_copy().start()
-
+    out_gate = pltpu.make_async_copy(mix, gate_grad_ref, l_sem.at[3])
+    out_gate.start()
     sides(3, round_x2)
-    sides(3, round_z)
 
     @pl.when(c < 31)
     def _():
         h_copy().wait_recv()
-        after_ref[...] = after[...]
-
-    @pl.when(c == 31)
-    def _():
-        after_ref[...] = jnp.zeros_like(after_ref)
-
+
+    def fy_copy(d):
+        return remote(fsum.at[(y + d) % 4], fy.at[d - 1], f_send.at[d], f_recv.at[d], ctx=at_y(d))
+
+    def fx_copy(d):
+        return remote(fxs.at[(x + d) % 4], fx.at[d - 1], f_send.at[4 + d], f_recv.at[4 + d], ctx=at_x(d))
+
+    def fz_copy():
+        return remote(fzs, fz, f_send.at[0], f_recv.at[0], ctx=partner)
+
+    for d in (2, 1, 3, 0):
+        def filter_back(i, carry):
+            g = 4 * i + (y + d) % 4
+            rows = pl.ds(pl.multiple_of(g * 16, 16), 16)
+            kv_grads, taps_part = back_group(
+                before, kv, work, after, rows, taps[g % 16, g // 16].astype(F32), part
+            )
+            for b in range(8):
+                kv_grad_ref[rows, b * 128 : (b + 1) * 128] = kv_grads[b].astype(BF)
+            fsum[(y + d) % 4, i % 4, i // 4] = taps_part
+            return carry
+
+        lax.fori_loop(0, 8, filter_back, 0)
+        if d:
+            fy_copy(d).start()
+        if d == 2:
+            sides(3, round_z)
+
+    for d in (2, 1, 3):
+        fy_copy(d).wait_recv()
+    fxs[...] = fsum[y] + fy[0] + fy[1] + fy[2]
+    for d in (2, 1, 3):
+        fx_copy(d).start()
     z_copy().wait_recv()
     w_grad_ref[...] = (prod[4 * zh + x, y] + zb[...].astype(F32)) * scale
+    for d in (2, 1, 3):
+        fx_copy(d).wait_recv()
+    fzs[...] = fxs[x, 1 - zh] + fx[0, 1 - zh] + fx[1, 1 - zh] + fx[2, 1 - zh]
+    fz_copy().start()
+    mine = fxs[x, zh] + fx[0, zh] + fx[1, zh] + fx[2, zh]
+    fz_copy().wait_recv()
+    filt_grad_ref[...] = (mine + fz[...]) * scale
+    out_gate.wait()
 
     def sent_blocks(p, carry):
         for ch in range(NCH):
@@ -495,20 +572,33 @@
     def _():
         h_copy().wait_send()
 
-
-def exchange(out_grad, wt, gated, gate, mixed, scale):
+    @pl.when(c < 31)
+    def _():
+        b_copy().wait_send()
+
+    tz_copy().wait_send()
+    fz_copy().wait_send()
+    for d in (1, 2, 3):
+        ty_copy(d).wait_send()
+        tx_copy(d).wait_send()
+        fy_copy(d).wait_send()
+        fx_copy(d).wait_send()
+
+
+def exchange(out_grad, w_out, gate, kv, filters, scale):
     vmem = pl.BlockSpec(memory_space=pltpu.VMEM)
+    hbm = pl.BlockSpec(memory_space=pl.ANY)
     dma = pltpu.SemaphoreType.DMA
     return pl.pallas_call(
         functools.partial(exchange_kernel, scale=scale),
         out_shape=[
             jax.ShapeDtypeStruct((512, 1024), F32),
             jax.ShapeDtypeStruct((512, 1024), BF),
-            jax.ShapeDtypeStruct((512, 128), BF),
+            jax.ShapeDtypeStruct((16, 128), F32),
             jax.ShapeDtypeStruct((128, 512), F32),
         ],
-        in_specs=[vmem] * 5,
-        out_specs=[vmem] * 4,
+        in_specs=[hbm, vmem, hbm, hbm, vmem],
+        out_specs=[hbm, vmem, vmem, vmem],
         scratch_shapes=[
             pltpu.VMEM((8, 512, 1024), BF),
             pltpu.VMEM((16, 2, 512, 128), BF),
@@ -517,6 +607,20 @@
             pltpu.VMEM((512, 1024), F32),
             pltpu.VMEM((512, 128), BF),
             pltpu.VMEM((512, 128), BF),
+            pltpu.VMEM((512, 128), BF),
+            pltpu.VMEM((512, 128), BF),
+            pltpu.VMEM((16, 2, 16, 128), BF),
+            pltpu.VMEM((512, 1024), BF),
+            pltpu.VMEM((512, 1024), BF),
+            pltpu.VMEM((512, 1024), BF),
+            pltpu.VMEM((512, 1024), BF),
+            pltpu.VMEM((16, 8, 128), F32),
+            pltpu.VMEM((4, 4, 2, 16, 128), F32),
+            pltpu.VMEM((3, 4, 2, 16, 128), F32),
+            pltpu.VMEM((3, 2, 16, 128), F32),
+            pltpu.VMEM((16, 128), F32),
+            pltpu.VMEM((4, 2, 16, 128), F32),
+            pltpu.VMEM((16, 128), F32),
             pltpu.VMEM((8, 2, 128, 256), BF),
             pltpu.VMEM((8, 2, 128, 256), BF),
             pltpu.VMEM((8, 2, 128, 512), BF),
@@ -529,25 +633,19 @@
             pltpu.VMEM((128, 512), BF),
             dma((4, NCH, 2)), dma((4, NCH)), dma((4, NCH)), dma((4, NCH)), dma((12,)), dma((12,)),
             dma((8, 2)), dma((8, 2)), dma((8, 2)), dma((8, 2)), dma((8, 2)), dma((8, 2)), dma((8,)), dma((8, 2)),
-            dma, dma, dma, dma, dma((2,)),
+            dma, dma, dma, dma, dma, dma, dma((8,)), dma((8,)), dma((8,)), dma((8,)), dma((4,)),
         ],
         compiler_params=pltpu.CompilerParams(
             collective_id=0, has_side_effects=True, vmem_limit_bytes=60 << 20
         ),
-    )(out_grad, wt, gated, gate, mixed)
+    )(out_grad, w_out, gate, kv, filters)
 
 
 def on_device(out_grad, gate_values, kv_product, w_out, filters):
-    ctx_count = lax.axis_size("ctx")
-    norm_scale = 1.0 / math.sqrt(ctx_count * out_grad.shape[1])
-    own_filters = filters.reshape(filters.shape[2:])
-    taps = lax.all_gather(own_filters, "ctx", axis=0, tiled=True)
-    before = lax.ppermute(kv_product[:, -128:], "ctx", [(i, i + 1) for i in range(ctx_count - 1)])
-    mixed, gated = conv_a(kv_product, before, gate_values, taps)
-    gate_grad, conv_grad, after, w_grad = exchange(out_grad, w_out.T, gated, gate_values, mixed, norm_scale)
-    turned = jnp.roll(taps[:, ::-1], 1, axis=1)
-    kv_grad, filter_part = conv_b(kv_product, before, conv_grad, after, turned)
-    filter_grad = lax.psum_scatter(filter_part, "ctx", scatter_dimension=0, tiled=True) * norm_scale
+    scale = 1.0 / math.sqrt(lax.axis_size("ctx") * out_grad.shape[1])
+    gate_grad, kv_grad, filter_grad, w_grad = exchange(
+        out_grad, w_out, gate_values, kv_product, filters.reshape(filters.shape[2:]), scale
+    )
     return (gate_grad, kv_grad, filter_grad.reshape(filters.shape), w_grad)
 
 

time: 531 us -> 171 us (0.32)
  the two profiles are of different devices: /device:TPU:32 before, /device:TPU:24 now
where the time goes in v2:
time: 171 us
  Pallas kernels  165 us (96%)
  local copies, waits for them, and re-layouts  5.53 us (3%)
    pallas_call x1, Pallas kernels, exchange(): pl.pallas_call(functools.partial(exchange_kernel, scale=scale), out_shape...  165 us
    unnamed x10, local copies, waits for them, and re-layouts  5.53 us

profile of v2, /device:TPU:24, one launch (start us, length us, event | category | flops | bytes accessed | tf_op | source)
XLA Modules:
  0.0 170.8 jit_solution(9368275375361841397)
XLA Ops:
  0.6 164.6 %shard_map.84 = (f32[512,1024]{1,0:T(8,128)}, bf16[512,1024]{1,0:T(8,128)(2,1)}, f32[16,128]{1,0:T(8,128)}, f32[128,512]{1,0:T(8,128)}) custom-call(bf16[512,1024]{1,0:T(8,128)(2,1)} %g_ref.1, bf16[128,512]{1,0:T(8,128)(2,1)} %w_ref.1, bf16[512,1024]{1,0:T(8,128)(2,1)} %gate_hbm.1, bf16[512,1024]{1,0:T(8,128)(2,1)} %kv_hbm.1, bf16[16,128]{1,0:T(8,128)(2,1)} %bitcast.3), custom_call_target="tpu_custom_call" | custom-call | tf_op jit(solution)/shard_map/pallas_call | solution.py:592
  165.3 0.0 copy-start
  165.3 0.0 copy-start.2
  165.3 3.2 %copy.13 = f32[512,1024]{1,0:T(8,128)} copy(f32[512,1024]{1,0:T(8,128)} %get-tuple-element.16) | data formatting | bytes 4194304
  168.5 0.0 copy-done
  168.5 0.0 copy-start.1
  168.5 1.0 copy.14
  169.5 0.0 copy-done.2
  169.5 0.6 copy.15
  170.1 0.0 copy-done.1
  170.1 0.7 copy.16
Async XLA Ops:
  165.3 3.3 %copy-start = (bf16[512,1024]{1,0:T(8,128)(2,1)S(1)}, bf16[512,1024]{1,0:T(8,128)(2,1)}, u32[]{:S(2)}) copy-start(bf16[512,1024]{1,0:T(8,128)(2,1)} %get-tuple-element.17) | copy-start | bytes 3145732
  165.3 4.2 %copy-start.2 = (f32[16,128]{1,0:T(8,128)S(1)}, f32[16,128]{1,0:T(8,128)}, u32[]{:S(2)}) copy-start(f32[16,128]{1,0:T(8,128)} %get-tuple-element.10) | copy-start | bytes 24580
  168.5 1.6 copy-start.1

commit v3 on v2

--- a/solution.py
+++ b/solution.py
@@ -92,7 +92,7 @@
     g_ref, w_ref, gate_hbm, kv_hbm, filt_ref,
     gate_grad_ref, kv_grad_ref, filt_grad_ref, w_grad_ref,
     gbuf, wbuf, gated_t, prod, mix, head, after, tail, before, taps,
-    gate, kv, mixed, work, part, fsum, fy, fx, fz, fxs, fzs,
+    gate, kv, mixed, work, part, fsum, fin,
     y1s, y1b, y2s, y2b, x1s, x1b, x2s, x2b, zs, zb,
     g_send, g_recv, s_send, s_recv, w_send, w_recv,
     y1_send, y1_recv, y2_send, y2_recv, x1_send, x1_recv, x2_send, x2_recv, z_send, z_recv,
@@ -126,20 +126,12 @@
         greet(fsdp=left)
 
     greet(fsdp=twin)
-    for d in (1, 2, 3):
-        greet(ctx=at_y(d))
-    for d in (1, 2, 3):
-        greet(ctx=at_x(d))
-    greet(ctx=partner)
-
-    @pl.when(c < 31)
-    def _():
-        greet(ctx=c + 1)
-
-    @pl.when(c > 0)
-    def _():
-        greet(ctx=c - 1)
-
+
+    def greet_peer(i, carry):
+        greet(ctx=(c + i) % 32)
+        return carry
+
+    lax.fori_loop(1, 32, greet_peer, 0)
     own_g = pltpu.make_async_copy(g_ref, gbuf.at[f], l_sem.at[0])
     own_kv = pltpu.make_async_copy(kv_hbm, kv, l_sem.at[1])
     own_gate = pltpu.make_async_copy(gate_hbm, gate, l_sem.at[2])
@@ -159,7 +151,7 @@
     def _():
         after[...] = jnp.zeros_like(after)
 
-    count = jnp.where(z < 3, 1, 0) + jnp.where(z > 0, 1, 0) + jnp.where(c < 31, 1, 0) + jnp.where(c > 0, 1, 0) + 8
+    count = jnp.where(z < 3, 1, 0) + jnp.where(z > 0, 1, 0) + 32
     pl.semaphore_wait(barrier, count)
     own_g.wait()
 
@@ -167,8 +159,7 @@
 
     def g_copy(p, ch, way):
         block = gbuf.at[2 * p + k, pl.ds(ch * span, span)]
-        to = right if way == 0 else left
-        return remote(block, block, g_send.at[p, ch, way], g_recv.at[p, ch], fsdp=to)
+        return remote(block, block, g_send.at[p, ch, way], g_recv.at[p, ch], fsdp=right - 4 * way)
 
     def twin_copy(p, ch):
         block = gbuf.at[2 * p + k, pl.ds(ch * span, span)]
@@ -193,19 +184,15 @@
     def b_copy():
         return remote(tail, before, b_send, b_recv, ctx=c + 1)
 
-    def tz_copy():
+    def t_copy(i):
         block = taps.at[xy, zh]
-        return remote(block, block, t_send.at[0], t_recv.at[0], ctx=partner)
-
-    def ty_copy(d):
-        block = taps.at[xy]
-        return remote(block, block, t_send.at[d], t_recv.at[d], ctx=at_y(d))
-
-    def tx_copy(d):
-        block = taps.at[pl.ds(4 * x, 4)]
-        return remote(block, block, t_send.at[4 + d], t_recv.at[4 + d], ctx=at_x(d))
-
-    tz_copy().start()
+        return remote(block, block, t_send.at[i], t_recv.at[i], ctx=(c + i) % 32)
+
+    def send_taps(i, carry):
+        t_copy(i).start()
+        return carry
+
+    lax.fori_loop(1, 32, send_taps, 0)
 
     @pl.when(c < 31)
     def _():
@@ -225,23 +212,18 @@
 
     mix[...] = jnp.zeros_like(mix)
 
-    tz_copy().wait_recv()
-    for d in (1, 3, 2):
-        ty_copy(d).start()
-    for d in (1, 3, 2):
-        ty_copy(d).wait_recv()
-    for d in (1, 3, 2):
-        tx_copy(d).start()
+    def have_taps(i, carry):
+        t_copy(i).wait_recv()
+        return carry
+
+    lax.fori_loop(1, 32, have_taps, 0)
     wz_copy().wait_recv()
     for d in (1, 3, 2):
         wy_copy(d).start()
-    for d in (1, 3, 2):
-        tx_copy(d).wait_recv()
 
     @pl.when(c > 0)
     def _():
-        b_copy_in = b_copy()
-        b_copy_in.wait_recv()
+        b_copy().wait_recv()
 
     own_gate.wait()
 
@@ -257,11 +239,44 @@
             work[rows, cols] = (gate[rows, cols].astype(F32) * narrow.astype(F32)).astype(BF)
         return carry
 
+    def sides(s, act):
+        if s == 0:
+            act(z)
+            return
+
+        def one(side, carry):
+            p = z - s + 2 * s * side
+
+            @pl.when((p >= 0) & (p < 4))
+            def _():
+                act(p)
+
+            return carry
+
+        lax.fori_loop(0, 2, one, 0)
+
+    def pass_on(s, ch):
+        def act(p):
+            g_copy(p, ch, 0).wait_recv()
+
+            @pl.when((p < z) & (z < 3))
+            def _():
+                g_copy(p, ch, 0).start()
+
+            @pl.when((p > z) & (z > 0))
+            def _():
+                g_copy(p, ch, 1).start()
+
+            twin_copy(p, ch).start()
+
+        sides(s, act)
+
     lax.fori_loop(0, 16, filter_forward, 0)
     for d in (1, 3, 2):
         wy_copy(d).wait_recv()
     for d in (1, 3):
         wx_copy(d).start()
+    pass_on(1, 0)
     lax.fori_loop(16, 32, filter_forward, 0)
 
     def turn(i, carry):
@@ -381,78 +396,39 @@
                     zs[...] = total.astype(BF)
                     z_copy().start()
 
-    def sides(s, act):
-        @pl.when(z >= s)
-        def _():
-            act(z - s)
-
-        @pl.when((s > 0) & (z + s < 4))
-        def _():
-            act(z + s)
-
-    def step(s, carry):
+    def arrive(p):
         for ch in range(NCH):
-            @pl.when((s > 0) & (z >= s))
-            def _():
-                g_copy(z - s, ch, 0).wait_recv()
-
-                @pl.when(z < 3)
-                def _():
-                    g_copy(z - s, ch, 0).start()
-
-                twin_copy(z - s, ch).start()
-
-            @pl.when((s > 0) & (z + s < 4))
-            def _():
-                g_copy(z + s, ch, 1).wait_recv()
-
-                @pl.when(z > 0)
-                def _():
-                    g_copy(z + s, ch, 1).start()
-
-                twin_copy(z + s, ch).start()
-
-        def arrive(p):
-            for ch in range(NCH):
-                twin_copy(p, ch).wait_recv()
-            multiply_rows(p)
-
-        sides(s, arrive)
-
-        @pl.when(s > 0)
-        def _():
-            sides(s - 1, round_x2)
-
-        @pl.when(s == 1)
-        def _():
-            wx_copy(1).wait_recv()
-            wf_copy(1).start()
-            wx_copy(3).wait_recv()
-            wf_copy(3).start()
-
-        @pl.when(s == 2)
-        def _():
-            wf_copy(1).wait_recv()
-            wf_copy(3).wait_recv()
-
-        @pl.when(s >= 2)
-        def _():
-            def late(q, carry):
-                sides(q, multiply_columns)
-                return carry
-
-            lax.fori_loop(jnp.where(s == 2, 0, 3), s + 1, late, 0)
-
-        sides(s, round_y2)
-
-        @pl.when(s > 0)
-        def _():
-            sides(s - 1, round_z)
-
-        sides(s, round_x1)
-        return carry
-
-    lax.fori_loop(0, 4, step, 0)
+            twin_copy(p, ch).wait_recv()
+        multiply_rows(p)
+
+    arrive(z)
+    sides(0, round_y2)
+    pass_on(1, 1)
+    sides(1, arrive)
+    sides(0, round_x1)
+    pass_on(2, 0)
+    sides(1, round_y2)
+    sides(0, round_x2)
+    wx_copy(1).wait_recv()
+    wf_copy(1).start()
+    wx_copy(3).wait_recv()
+    wf_copy(3).start()
+    pass_on(2, 1)
+    sides(2, arrive)
+    sides(1, round_x1)
+    sides(0, round_z)
+    pass_on(3, 0)
+    sides(2, round_y2)
+    sides(1, round_x2)
+    wf_copy(1).wait_recv()
+    wf_copy(3).wait_recv()
+    for s in (0, 1, 2):
+        sides(s, multiply_columns)
+    pass_on(3, 1)
+    sides(3, arrive)
+    sides(2, round_x1)
+    sides(1, round_z)
+    sides(3, multiply_columns)
 
     def h_copy():
         return remote(head, after, h_send, h_recv, ctx=c - 1)
@@ -478,53 +454,48 @@
     lax.fori_loop(0, 16, finish, 0)
     out_gate = pltpu.make_async_copy(mix, gate_grad_ref, l_sem.at[3])
     out_gate.start()
+    sides(3, round_y2)
+    sides(2, round_x2)
+
+    @pl.when(c < 31)
+    def _():
+        h_copy().wait_recv()
+
+    def f_copy(i):
+        return remote(fsum.at[(c + i) % 32], fin.at[i], f_send.at[i], f_recv.at[i], ctx=(c + i) % 32)
+
+    def filter_back(i, carry):
+        g = (c + i) % 32
+        rows = pl.ds(pl.multiple_of(g * 16, 16), 16)
+        kv_grads, taps_part = back_group(
+            before, kv, work, after, rows, taps[g % 16, g // 16].astype(F32), part
+        )
+        for b in range(8):
+            kv_grad_ref[rows, b * 128 : (b + 1) * 128] = kv_grads[b].astype(BF)
+        fsum[g] = taps_part
+
+        @pl.when(i < 32)
+        def _():
+            f_copy(i).start()
+
+        return carry
+
+    lax.fori_loop(1, 9, filter_back, 0)
+    sides(3, round_x1)
+    lax.fori_loop(9, 17, filter_back, 0)
     sides(3, round_x2)
-
-    @pl.when(c < 31)
-    def _():
-        h_copy().wait_recv()
-
-    def fy_copy(d):
-        return remote(fsum.at[(y + d) % 4], fy.at[d - 1], f_send.at[d], f_recv.at[d], ctx=at_y(d))
-
-    def fx_copy(d):
-        return remote(fxs.at[(x + d) % 4], fx.at[d - 1], f_send.at[4 + d], f_recv.at[4 + d], ctx=at_x(d))
-
-    def fz_copy():
-        return remote(fzs, fz, f_send.at[0], f_recv.at[0], ctx=partner)
-
-    for d in (2, 1, 3, 0):
-        def filter_back(i, carry):
-            g = 4 * i + (y + d) % 4
-            rows = pl.ds(pl.multiple_of(g * 16, 16), 16)
-            kv_grads, taps_part = back_group(
-                before, kv, work, after, rows, taps[g % 16, g // 16].astype(F32), part
-            )
-            for b in range(8):
-                kv_grad_ref[rows, b * 128 : (b + 1) * 128] = kv_grads[b].astype(BF)
-            fsum[(y + d) % 4, i % 4, i // 4] = taps_part
-            return carry
-
-        lax.fori_loop(0, 8, filter_back, 0)
-        if d:
-            fy_copy(d).start()
-        if d == 2:
-            sides(3, round_z)
-
-    for d in (2, 1, 3):
-        fy_copy(d).wait_recv()
-    fxs[...] = fsum[y] + fy[0] + fy[1] + fy[2]
-    for d in (2, 1, 3):
-        fx_copy(d).start()
+    sides(2, round_z)
+    lax.fori_loop(17, 25, filter_back, 0)
+    sides(3, round_z)
+    lax.fori_loop(25, 33, filter_back, 0)
     z_copy().wait_recv()
     w_grad_ref[...] = (prod[4 * zh + x, y] + zb[...].astype(F32)) * scale
-    for d in (2, 1, 3):
-        fx_copy(d).wait_recv()
-    fzs[...] = fxs[x, 1 - zh] + fx[0, 1 - zh] + fx[1, 1 - zh] + fx[2, 1 - zh]
-    fz_copy().start()
-    mine = fxs[x, zh] + fx[0, zh] + fx[1, zh] + fx[2, zh]
-    fz_copy().wait_recv()
-    filt_grad_ref[...] = (mine + fz[...]) * scale
+
+    def gather_taps(i, total):
+        f_copy(i).wait_recv()
+        return total + fin[i]
+
+    filt_grad_ref[...] = lax.fori_loop(1, 32, gather_taps, fsum[c]) * scale
     out_gate.wait()
 
     def sent_blocks(p, carry):
@@ -576,13 +547,12 @@
     def _():
         b_copy().wait_send()
 
-    tz_copy().wait_send()
-    fz_copy().wait_send()
-    for d in (1, 2, 3):
-        ty_copy(d).wait_send()
-        tx_copy(d).wait_send()
-        fy_copy(d).wait_send()
-        fx_copy(d).wait_send()
+    def sent_small(i, carry):
+        t_copy(i).wait_send()
+        f_copy(i).wait_send()
+        return carry
+
+    lax.fori_loop(1, 32, sent_small, 0)
 
 
 def exchange(out_grad, w_out, gate, kv, filters, scale):
@@ -615,12 +585,8 @@
             pltpu.VMEM((512, 1024), BF),
             pltpu.VMEM((512, 1024), BF),
             pltpu.VMEM((16, 8, 128), F32),
-            pltpu.VMEM((4, 4, 2, 16, 128), F32),
-            pltpu.VMEM((3, 4, 2, 16, 128), F32),
-            pltpu.VMEM((3, 2, 16, 128), F32),
-            pltpu.VMEM((16, 128), F32),
-            pltpu.VMEM((4, 2, 16, 128), F32),
-            pltpu.VMEM((16, 128), F32),
+            pltpu.VMEM((32, 16, 128), F32),
+            pltpu.VMEM((32, 16, 128), F32),
             pltpu.VMEM((8, 2, 128, 256), BF),
             pltpu.VMEM((8, 2, 128, 256), BF),
             pltpu.VMEM((8, 2, 128, 512), BF),
@@ -633,7 +599,7 @@
             pltpu.VMEM((128, 512), BF),
             dma((4, NCH, 2)), dma((4, NCH)), dma((4, NCH)), dma((4, NCH)), dma((12,)), dma((12,)),
             dma((8, 2)), dma((8, 2)), dma((8, 2)), dma((8, 2)), dma((8, 2)), dma((8, 2)), dma((8,)), dma((8, 2)),
-            dma, dma, dma, dma, dma, dma, dma((8,)), dma((8,)), dma((8,)), dma((8,)), dma((4,)),
+            dma, dma, dma, dma, dma, dma, dma((32,)), dma((32,)), dma((32,)), dma((32,)), dma((4,)),
         ],
         compiler_params=pltpu.CompilerParams(
             collective_id=0, has_side_effects=True, vmem_limit_bytes=60 << 20

time: 171 us -> 152 us (0.89)
  the two profiles are of different devices: /device:TPU:24 before, /device:TPU:7 now
where the time goes in v3:
time: 152 us
  Pallas kernels  146 us (96%)
  local copies, waits for them, and re-layouts  5.53 us (4%)
    pallas_call x1, Pallas kernels, exchange(): pl.pallas_call(functools.partial(exchange_kernel, scale=scale), out_shape...  146 us
    unnamed x10, local copies, waits for them, and re-layouts  5.53 us

profile of v3, /device:TPU:7, one launch (start us, length us, event | category | flops | bytes accessed | tf_op | source)
XLA Modules:
  0.0 152.0 jit_solution(17083658341968544096)
XLA Ops:
  0.6 145.8 %shard_map.84 = (f32[512,1024]{1,0:T(8,128)}, bf16[512,1024]{1,0:T(8,128)(2,1)}, f32[16,128]{1,0:T(8,128)}, f32[128,512]{1,0:T(8,128)}) custom-call(bf16[512,1024]{1,0:T(8,128)(2,1)} %g_ref.1, bf16[128,512]{1,0:T(8,128)(2,1)} %w_ref.1, bf16[512,1024]{1,0:T(8,128)(2,1)} %gate_hbm.1, bf16[512,1024]{1,0:T(8,128)(2,1)} %kv_hbm.1, bf16[16,128]{1,0:T(8,128)(2,1)} %bitcast.3), custom_call_target="tpu_custom_call" | custom-call | tf_op jit(solution)/shard_map/pallas_call | solution.py:562
  146.4 0.0 copy-start
  146.4 0.0 copy-start.2
  146.5 3.2 %copy.13 = f32[512,1024]{1,0:T(8,128)} copy(f32[512,1024]{1,0:T(8,128)} %get-tuple-element.16) | data formatting | bytes 4194304
  149.7 0.0 copy-done
  149.7 0.0 copy-start.1
  149.7 1.0 copy.14
  150.7 0.0 copy-done.2
  150.7 0.6 copy.15
  151.3 0.0 copy-done.1
  151.3 0.7 copy.16
Async XLA Ops:
  146.4 3.3 %copy-start = (bf16[512,1024]{1,0:T(8,128)(2,1)S(1)}, bf16[512,1024]{1,0:T(8,128)(2,1)}, u32[]{:S(2)}) copy-start(bf16[512,1024]{1,0:T(8,128)(2,1)} %get-tuple-element.17) | copy-start | bytes 3145732
  146.4 4.2 %copy-start.2 = (f32[16,128]{1,0:T(8,128)S(1)}, f32[16,128]{1,0:T(8,128)}, u32[]{:S(2)}) copy-start(f32[16,128]{1,0:T(8,128)} %get-tuple-element.10) | copy-start | bytes 24580
  149.7 1.6 %copy-start.1 = (f32[128,512]{1,0:T(8,128)S(1)}, f32[128,512]{1,0:T(8,128)}, u32[]{:S(2)}) copy-start(f32[128,512]{1,0:T(8,128)} %get-tuple-element.19) | copy-start | bytes 786436

commit v4 on v3

--- a/solution.py
+++ b/solution.py
@@ -47,38 +47,50 @@
     return [jnp.concatenate(o, axis=0) for o in out]
 
 
-def back_group(before, kv, grad, after, rows, taps, part):
-    xs = [before[rows, :]] + [kv[rows, b * 128 : (b + 1) * 128] for b in range(8)]
-    gs = [grad[rows, b * 128 : (b + 1) * 128] for b in range(8)] + [after[rows, :]]
+def back_group(before, kv, grad, after, rows, taps, part, kv_grad, with_kv, with_taps):
+    gs = [grad[rows, b * 128 : (b + 1) * 128] for b in range(8)]
     row_at = lax.broadcasted_iota(jnp.int32, (128, 128), 0)
     lane_at = lax.broadcasted_iota(jnp.int32, (128, 128), 1)
-    lhs = stack_blocks(gs)
-    x_turned = stack_blocks(xs).astype(F32).T.astype(BF)
-    wide = jnp.concatenate(gs[:8], axis=0).astype(F32)
+    if with_kv:
+        lhs = stack_blocks(gs + [after[rows, :]])
+    if with_taps:
+        xs = [before[rows, :]] + [kv[rows, b * 128 : (b + 1) * 128] for b in range(8)]
+        x_turned = stack_blocks(xs).astype(F32).T.astype(BF)
+        wide = jnp.concatenate(gs, axis=0).astype(F32)
     out = [[None, None] for _ in range(8)]
     for pair in range(8):
         band_rows, own_grad = [], []
         for ch in (2 * pair, 2 * pair + 1):
-            far, near = bands(taps[ch : ch + 1, :])
-            band_rows.append(jnp.concatenate([near, far], axis=1))
-            own_grad.append(jnp.where(row_at % 16 == ch, wide, 0.0).astype(BF))
-        product = lax.dot_general(
-            lhs, jnp.concatenate(band_rows, axis=0), (((1,), (1,)), ((), ())), preferred_element_type=F32
-        )
-        outer = jnp.dot(x_turned, jnp.concatenate(own_grad, axis=1), preferred_element_type=F32)
+            if with_kv:
+                far, near = bands(taps[ch : ch + 1, :])
+                band_rows.append(jnp.concatenate([near, far], axis=1))
+            if with_taps:
+                own_grad.append(jnp.where(row_at % 16 == ch, wide, 0.0).astype(BF))
+        if with_kv:
+            product = lax.dot_general(
+                lhs, jnp.concatenate(band_rows, axis=0), (((1,), (1,)), ((), ())), preferred_element_type=F32
+            )
+        if with_taps:
+            outer = jnp.dot(x_turned, jnp.concatenate(own_grad, axis=1), preferred_element_type=F32)
         for i in range(2):
             ch = 2 * pair + i
-            keep_own(out, product, ch, i)
-            cols = slice(i * 128, (i + 1) * 128)
-            both = jnp.where(lane_at >= row_at, outer[128:, cols], outer[:128, cols])
-            acc = both[0:8]
-            for v in range(1, 16):
-                acc = acc + pltpu.roll(both[8 * v : 8 * v + 8], 128 - 8 * v, 1)
-            part[ch] = acc
-    taps_part = part[:, 0, :]
-    for u in range(1, 8):
-        taps_part = taps_part + pltpu.roll(part[:, u, :], 128 - u, 1)
-    return [jnp.concatenate(o, axis=0) for o in out], taps_part
+            if with_kv:
+                keep_own(out, product, ch, i)
+            if with_taps:
+                cols = slice(i * 128, (i + 1) * 128)
+                both = jnp.where(lane_at >= row_at, outer[128:, cols], outer[:128, cols])
+                acc = both[0:8]
+                for v in range(1, 16):
+                    acc = acc + pltpu.roll(both[8 * v : 8 * v + 8], 128 - 8 * v, 1)
+                part[ch] = acc
+    if with_kv:
+        for b in range(8):
+            kv_grad[rows, b * 128 : (b + 1) * 128] = jnp.concatenate(out[b], axis=0).astype(BF)
+    if with_taps:
+        taps_part = part[:, 0, :]
+        for u in range(1, 8):
+            taps_part = taps_part + pltpu.roll(part[:, u, :], 128 - u, 1)
+        return taps_part
 
 
 NCH = 2
@@ -138,8 +150,11 @@
     own_kv.start()
     own_g.start()
     own_gate.start()
-    wbuf[xy, zh] = w_ref[...].astype(F32).T.astype(BF)
-    taps[xy, zh] = filt_ref[...]
+    turned = w_ref[...].astype(F32).T.astype(BF)
+    home = (xy, 4 * y + x)
+    for h in range(2):
+        wbuf[h, home[h], zh] = turned[256 * h : 256 * h + 256]
+    taps[c] = filt_ref[...]
     own_kv.wait()
     tail[...] = kv[:, 896:]
 
@@ -163,30 +178,39 @@
 
     def twin_copy(p, ch):
         block = gbuf.at[2 * p + k, pl.ds(ch * span, span)]
-        return remote(block, block, s_send.at[p, ch], s_recv.at[p, ch], fsdp=twin)
-
-    def wz_copy():
-        block = wbuf.at[xy, zh]
-        return remote(block, block, w_send.at[0], w_recv.at[0], ctx=partner)
-
-    def wy_copy(d):
-        block = wbuf.at[xy]
-        return remote(block, block, w_send.at[d], w_recv.at[d], ctx=at_y(d))
-
-    def wx_copy(d):
-        block = wbuf.at[pl.ds(4 * x, 4)]
-        return remote(block, block, w_send.at[4 + d], w_recv.at[4 + d], ctx=at_x(d))
-
-    def wf_copy(d):
-        block = wbuf.at[pl.ds(4 * ((x - d) % 4) + (0 if d == 1 else 2), 2)]
-        return remote(block, block, w_send.at[8 + d], w_recv.at[8 + d], ctx=at_x(d))
+        return remote(block, block, s_send, s_recv.at[p, ch], fsdp=twin)
+
+    across, along = (at_y, at_x), (at_x, at_y)
+    line = (x, y)
+
+    def w_remote(block, n, to):
+        return remote(block, block, w_send.at[n], w_recv.at[n], ctx=to)
+
+    def wz_copy(h):
+        return w_remote(wbuf.at[h, home[h], zh], h, partner)
+
+    def w1_copy(h, d):
+        return w_remote(wbuf.at[h, home[h]], 2 + 4 * h + d, across[h](d))
+
+    def w2_copy(h, d):
+        return w_remote(wbuf.at[h, pl.ds(4 * line[h], 4)], 10 + 4 * h + d, along[h](d))
+
+    def w3_copy(h, d):
+        first = 4 * ((line[h] - d) % 4) + (0 if d == 1 else 2)
+        return w_remote(wbuf.at[h, pl.ds(first, 2)], 18 + 4 * h + d, along[h](d))
+
+    for h in range(2):
+        wz_copy(h).start()
 
     def b_copy():
         return remote(tail, before, b_send, b_recv, ctx=c + 1)
 
     def t_copy(i):
-        block = taps.at[xy, zh]
-        return remote(block, block, t_send.at[i], t_recv.at[i], ctx=(c + i) % 32)
+        block = taps.at[c]
+        return remote(block, block, t_send, t_recv, ctx=(c + i) % 32)
+
+    def t_all():
+        return remote(taps.at[pl.ds(0, 31)], taps.at[pl.ds(0, 31)], t_send, t_recv, ctx=partner)
 
     def send_taps(i, carry):
         t_copy(i).start()
@@ -198,7 +222,6 @@
     def _():
         b_copy().start()
 
-    wz_copy().start()
     for ch in range(NCH):
         @pl.when(z < 3)
         def _():
@@ -212,14 +235,11 @@
 
     mix[...] = jnp.zeros_like(mix)
 
-    def have_taps(i, carry):
-        t_copy(i).wait_recv()
-        return carry
-
-    lax.fori_loop(1, 32, have_taps, 0)
-    wz_copy().wait_recv()
-    for d in (1, 3, 2):
-        wy_copy(d).start()
+    for h in range(2):
+        wz_copy(h).wait_recv()
+        for d in (1, 3, 2):
+            w1_copy(h, d).start()
+    t_all().wait_recv()
 
     @pl.when(c > 0)
     def _():
@@ -231,7 +251,7 @@
         rows = pl.ds(pl.multiple_of(g * 16, 16), 16)
         xs = [before[rows, :]] + [kv[rows, b * 128 : (b + 1) * 128] for b in range(8)]
         lhs = jnp.concatenate([jnp.concatenate([xs[b], xs[b + 1]], axis=1) for b in range(8)], axis=0)
-        outs = conv_group(taps[g % 16, g // 16].astype(F32), lhs, False)
+        outs = conv_group(taps[g].astype(F32), lhs, False)
         for b in range(8):
             cols = slice(b * 128, (b + 1) * 128)
             narrow = outs[b].astype(BF)
@@ -271,13 +291,15 @@
 
         sides(s, act)
 
-    lax.fori_loop(0, 16, filter_forward, 0)
-    for d in (1, 3, 2):
-        wy_copy(d).wait_recv()
-    for d in (1, 3):
-        wx_copy(d).start()
+    lax.fori_loop(0, 8, filter_forward, 0, unroll=2)
+    for h in range(2):
+        for d in (1, 3, 2):
+            w1_copy(h, d).wait_recv()
+        for d in (1, 3):
+            w2_copy(h, d).start()
+    lax.fori_loop(8, 20, filter_forward, 0, unroll=2)
     pass_on(1, 0)
-    lax.fori_loop(16, 32, filter_forward, 0)
+    lax.fori_loop(20, 32, filter_forward, 0, unroll=2)
 
     def turn(i, carry):
         cols = pl.ds(pl.multiple_of(i * 128, 128), 128)
@@ -287,16 +309,16 @@
     lax.fori_loop(0, 4, turn, 0)
 
     def y1_copy(b, j):
-        return remote(y1s.at[b, j], y1b.at[b, j], y1_send.at[b, j], y1_recv.at[b, j], ctx=at_y(1 if j == 0 else 3))
+        return remote(y1s.at[b, j], y1b.at[b, j], y1_send, y1_recv.at[b, j], ctx=at_y(1 if j == 0 else 3))
 
     def y2_copy(b, j):
-        return remote(y2s.at[b, j], y2b.at[b, j], y2_send.at[b, j], y2_recv.at[b, j], ctx=at_y(1 if j == 0 else 3))
+        return remote(y2s.at[b, j], y2b.at[b, j], y2_send, y2_recv.at[b, j], ctx=at_y(1 if j == 0 else 3))
 
     def x1_copy(b, j):
-        return remote(x1s.at[b, j], x1b.at[b, j], x1_send.at[b, j], x1_recv.at[b, j], ctx=at_x(1 if j == 0 else 3))
+        return remote(x1s.at[b, j], x1b.at[b, j], x1_send, x1_recv.at[b, j], ctx=at_x(1 if j == 0 else 3))
 
     def x2_copy(b, j):
-        return remote(x2s.at[b], x2b.at[b, j], x2_send.at[b], x2_recv.at[b, j], ctx=at_x(1 if j == 0 else 3))
+        return remote(x2s.at[b], x2b.at[b, j], x2_send, x2_recv.at[b, j], ctx=at_x(1 if j == 0 else 3))
 
     def z_copy():
         return remote(zs, zb, z_send, z_recv, ctx=partner)
@@ -319,15 +341,20 @@
                 y1_copy(b, j).start()
 
     def multiply_columns(p):
-        def tile(i, carry):
-            b, h, n = 2 * p + i // 4, (i // 2) % 2, i % 2
-            rows = pl.ds(pl.multiple_of(h * 256, 256), 256)
-            cols = pl.ds(pl.multiple_of(n * 512, 512), 512)
-            lhs = jnp.concatenate([wbuf[4 * (b % 4) + q, b // 4, rows, :] for q in range(4)], axis=1)
-            mix[rows, cols] += jnp.dot(lhs, gbuf[b, :, cols], preferred_element_type=F32)
-            return carry
-
-        lax.fori_loop(0, 8, tile, 0)
+        for h in range(2):
+            rows = slice(256 * h, 256 * h + 256)
+
+            def tile(n, carry):
+                cols = pl.ds(pl.multiple_of(n * 512, 512), 512)
+                slabs = []
+                for e in range(8):
+                    row, q = (2 * p + e // 4) % 4, e % 4
+                    slabs.append(wbuf[h, 4 * row + q if h == 0 else 4 * q + row, p // 2])
+                rhs = gbuf[pl.ds(2 * p, 2), :, cols].reshape(1024, 512)
+                mix[rows, cols] += jnp.dot(jnp.concatenate(slabs, axis=1), rhs, preferred_element_type=F32)
+                return carry
+
+            lax.fori_loop(0, 2, tile, 0)
 
     def round_y2(p):
         for i in range(2):
@@ -402,32 +429,31 @@
         multiply_rows(p)
 
     arrive(z)
+    pass_on(1, 1)
+    for h in range(2):
+        for d in (1, 3):
+            w2_copy(h, d).wait_recv()
+            w3_copy(h, d).start()
     sides(0, round_y2)
-    pass_on(1, 1)
     sides(1, arrive)
+    pass_on(2, 0)
     sides(0, round_x1)
-    pass_on(2, 0)
     sides(1, round_y2)
+    pass_on(2, 1)
     sides(0, round_x2)
-    wx_copy(1).wait_recv()
-    wf_copy(1).start()
-    wx_copy(3).wait_recv()
-    wf_copy(3).start()
-    pass_on(2, 1)
     sides(2, arrive)
     sides(1, round_x1)
-    sides(0, round_z)
     pass_on(3, 0)
     sides(2, round_y2)
     sides(1, round_x2)
-    wf_copy(1).wait_recv()
-    wf_copy(3).wait_recv()
+    for h in range(2):
+        for d in (1, 3):
+            w3_copy(h, d).wait_recv()
     for s in (0, 1, 2):
         sides(s, multiply_columns)
+    sides(2, round_x1)
     pass_on(3, 1)
     sides(3, arrive)
-    sides(2, round_x1)
-    sides(1, round_z)
     sides(3, multiply_columns)
 
     def h_copy():
@@ -457,45 +483,49 @@
     sides(3, round_y2)
     sides(2, round_x2)
 
-    @pl.when(c < 31)
-    def _():
-        h_copy().wait_recv()
-
     def f_copy(i):
-        return remote(fsum.at[(c + i) % 32], fin.at[i], f_send.at[i], f_recv.at[i], ctx=(c + i) % 32)
-
-    def filter_back(i, carry):
+        return remote(fsum.at[(c + i) % 32], fin.at[i], f_send, f_recv, ctx=(c + i) % 32)
+
+    def f_all():
+        return remote(fsum.at[pl.ds(0, 31)], fin.at[pl.ds(1, 31)], f_send, f_recv, ctx=partner)
+
+    def filter_back(i, with_kv, with_taps):
         g = (c + i) % 32
         rows = pl.ds(pl.multiple_of(g * 16, 16), 16)
-        kv_grads, taps_part = back_group(
-            before, kv, work, after, rows, taps[g % 16, g // 16].astype(F32), part
+        total = back_group(
+            before, kv, work, after, rows, taps[g].astype(F32), part, kv_grad_ref, with_kv, with_taps
         )
-        for b in range(8):
-            kv_grad_ref[rows, b * 128 : (b + 1) * 128] = kv_grads[b].astype(BF)
-        fsum[g] = taps_part
-
-        @pl.when(i < 32)
-        def _():
-            f_copy(i).start()
-
-        return carry
-
-    lax.fori_loop(1, 9, filter_back, 0)
+        if with_taps:
+            fsum[g] = total
+
+            @pl.when(i < 32)
+            def _():
+                f_copy(i).start()
+
+        return 0
+
+    lax.fori_loop(1, 9, lambda i, carry: filter_back(i, False, True), 0, unroll=2)
     sides(3, round_x1)
-    lax.fori_loop(9, 17, filter_back, 0)
+
+    @pl.when(c < 31)
+    def _():
+        h_copy().wait_recv()
+
+    lax.fori_loop(9, 17, lambda i, carry: filter_back(i, True, True), 0, unroll=2)
     sides(3, round_x2)
-    sides(2, round_z)
-    lax.fori_loop(17, 25, filter_back, 0)
+    for s in (0, 1, 2):
+        sides(s, round_z)
+    lax.fori_loop(17, 25, lambda i, carry: filter_back(i, True, True), 0, unroll=2)
     sides(3, round_z)
-    lax.fori_loop(25, 33, filter_back, 0)
+    lax.fori_loop(25, 33, lambda i, carry: filter_back(i, True, True), 0, unroll=2)
+    lax.fori_loop(1, 9, lambda i, carry: filter_back(i, True, False), 0, unroll=2)
     z_copy().wait_recv()
     w_grad_ref[...] = (prod[4 * zh + x, y] + zb[...].astype(F32)) * scale
-
-    def gather_taps(i, total):
-        f_copy(i).wait_recv()
-        return total + fin[i]
-
-    filt_grad_ref[...] = lax.fori_loop(1, 32, gather_taps, fsum[c]) * scale
+    f_all().wait_recv()
+    total = fsum[c]
+    for i in range(1, 32):
+        total = total + fin[i]
+    filt_grad_ref[...] = total * scale
     out_gate.wait()
 
     def sent_blocks(p, carry):
@@ -508,36 +538,26 @@
             def _():
                 g_copy(p, ch, 1).wait_send()
 
-            twin_copy(p, ch).wait_send()
         return carry
 
     lax.fori_loop(0, 4, sent_blocks, 0)
 
-    def sent_sums(b, carry):
-        for j in range(2):
-            y1_copy(b, j).wait_send()
-            y2_copy(b, j).wait_send()
-        role = (x - b) % 4
-
-        @pl.when(role == 2)
-        def _():
-            for j in range(2):
-                x1_copy(b, j).wait_send()
-
-        @pl.when(role % 2 == 1)
-        def _():
-            x2_copy(b, 0).wait_send()
-
-        return carry
-
-    lax.fori_loop(0, 8, sent_sums, 0)
+    def left(src, sem):
+        remote(src, src, sem, sem, ctx=partner).wait_send()
+
+    left(gbuf.at[pl.ds(0, 4)], s_send)
+    left(y1s, y1_send)
+    left(y2s, y2_send)
+    left(x1s.at[pl.ds(0, 2)], x1_send)
+    left(x2s.at[pl.ds(0, 4)], x2_send)
     z_copy().wait_send()
-    wz_copy().wait_send()
-    for d in (1, 2, 3):
-        wy_copy(d).wait_send()
-    for d in (1, 3):
-        wx_copy(d).wait_send()
-        wf_copy(d).wait_send()
+    for h in range(2):
+        wz_copy(h).wait_send()
+        for d in (1, 2, 3):
+            w1_copy(h, d).wait_send()
+        for d in (1, 3):
+            w2_copy(h, d).wait_send()
+            w3_copy(h, d).wait_send()
 
     @pl.when(c > 0)
     def _():
@@ -547,12 +567,8 @@
     def _():
         b_copy().wait_send()
 
-    def sent_small(i, carry):
-        t_copy(i).wait_send()
-        f_copy(i).wait_send()
-        return carry
-
-    lax.fori_loop(1, 32, sent_small, 0)
+    t_all().wait_send()
+    f_all().wait_send()
 
 
 def exchange(out_grad, w_out, gate, kv, filters, scale):
@@ -571,7 +587,7 @@
         out_specs=[hbm, vmem, vmem, vmem],
         scratch_shapes=[
             pltpu.VMEM((8, 512, 1024), BF),
-            pltpu.VMEM((16, 2, 512, 128), BF),
+            pltpu.VMEM((2, 16, 2, 256, 128), BF),
             pltpu.VMEM((1024, 512), BF),
             pltpu.VMEM((8, 4, 128, 512), F32),
             pltpu.VMEM((512, 1024), F32),
@@ -579,7 +595,7 @@
             pltpu.VMEM((512, 128), BF),
             pltpu.VMEM((512, 128), BF),
             pltpu.VMEM((512, 128), BF),
-            pltpu.VMEM((16, 2, 16, 128), BF),
+            pltpu.VMEM((32, 16, 128), BF),
             pltpu.VMEM((512, 1024), BF),
             pltpu.VMEM((512, 1024), BF),
             pltpu.VMEM((512, 1024), BF),
@@ -597,9 +613,9 @@
             pltpu.VMEM((8, 2, 128, 512), BF),
             pltpu.VMEM((128, 512), BF),
             pltpu.VMEM((128, 512), BF),
-            dma((4, NCH, 2)), dma((4, NCH)), dma((4, NCH)), dma((4, NCH)), dma((12,)), dma((12,)),
-            dma((8, 2)), dma((8, 2)), dma((8, 2)), dma((8, 2)), dma((8, 2)), dma((8, 2)), dma((8,)), dma((8, 2)),
-            dma, dma, dma, dma, dma, dma, dma((32,)), dma((32,)), dma((32,)), dma((32,)), dma((4,)),
+            dma((4, NCH, 2)), dma((4, NCH)), dma, dma((4, NCH)), dma((26,)), dma((26,)),
+            dma, dma((8, 2)), dma, dma((8, 2)), dma, dma((8, 2)), dma, dma((8, 2)),
+            dma, dma, dma, dma, dma, dma, dma, dma, dma, dma, dma((4,)),
         ],
         compiler_params=pltpu.CompilerParams(
             collective_id=0, has_side_effects=True, vmem_limit_bytes=60 << 20

time: 152 us -> 147 us (0.967)
  the two profiles are of different devices: /device:TPU:7 before, /device:TPU:23 now
where the time goes in v4:
time: 147 us
  Pallas kernels  141 us (96%)
  local copies, waits for them, and re-layouts  5.53 us (4%)
    pallas_call x1, Pallas kernels, exchange(): pl.pallas_call(functools.partial(exchange_kernel, scale=scale), out_shape...  141 us
    unnamed x10, local copies, waits for them, and re-layouts  5.53 us

profile of v4, /device:TPU:23, one launch (start us, length us, event | category | flops | bytes accessed | tf_op | source)
XLA Modules:
  0.0 147.1 jit_solution(12178320413503779556)
XLA Ops:
  0.6 140.9 %shard_map.84 = (f32[512,1024]{1,0:T(8,128)}, bf16[512,1024]{1,0:T(8,128)(2,1)}, f32[16,128]{1,0:T(8,128)}, f32[128,512]{1,0:T(8,128)}) custom-call(bf16[512,1024]{1,0:T(8,128)(2,1)} %g_ref.1, bf16[128,512]{1,0:T(8,128)(2,1)} %w_ref.1, bf16[512,1024]{1,0:T(8,128)(2,1)} %gate_hbm.1, bf16[512,1024]{1,0:T(8,128)(2,1)} %kv_hbm.1, bf16[16,128]{1,0:T(8,128)(2,1)} %bitcast.3), custom_call_target="tpu_custom_call" | custom-call | tf_op jit(solution)/shard_map/pallas_call | solution.py:578
  141.5 0.0 copy-start
  141.5 0.0 copy-start.2
  141.5 3.2 %copy.13 = f32[512,1024]{1,0:T(8,128)} copy(f32[512,1024]{1,0:T(8,128)} %get-tuple-element.16) | data formatting | bytes 4194304
  144.8 0.0 copy-done
  144.8 0.0 copy-start.1
  144.8 1.0 copy.14
  145.7 0.0 copy-done.2
  145.8 0.6 copy.15
  146.3 0.0 copy-done.1
  146.4 0.7 copy.16
Async XLA Ops:
  141.5 3.3 %copy-start = (bf16[512,1024]{1,0:T(8,128)(2,1)S(1)}, bf16[512,1024]{1,0:T(8,128)(2,1)}, u32[]{:S(2)}) copy-start(bf16[512,1024]{1,0:T(8,128)(2,1)} %get-tuple-element.17) | copy-start | bytes 3145732
  141.5 4.2 %copy-start.2 = (f32[16,128]{1,0:T(8,128)S(1)}, f32[16,128]{1,0:T(8,128)}, u32[]{:S(2)}) copy-start(f32[16,128]{1,0:T(8,128)} %get-tuple-element.10) | copy-start | bytes 24580
  144.8 1.6 %copy-start.1 = (f32[128,512]{1,0:T(8,128)S(1)}, f32[128,512]{1,0:T(8,128)}, u32[]{:S(2)}) copy-start(f32[128,512]{1,0:T(8,128)} %get-tuple-element.19) | copy-start | bytes 786436
